TPU v7x, 256 devices: a whole 4x4x8 slice. The times are simulated.
256 devices in a mesh: ep: 64 (over y_lo, z, x), fsdp: 4 (over y_hi, core).
Axes of the slice: x: 4, y: 4 (y_hi: 2, y_lo: 2; y = y_hi * 2 + y_lo), z: 8, core: 2. Of those that a mesh axis runs over, the one named last changes fastest.
Arguments:
- tokens: bfloat16 [12288, 4096], P(('ep', 'fsdp')), may hold values from -6 to 6
- expert_ids: int32 [12288, 8], P(('ep', 'fsdp')), may hold values from 0 to 63, all different within a row; in each aligned block of 48 rows (0 to 47, 48 to 95, ...) at most 9 rows name the same one
- gate_values: float32 [12288, 8], P(('ep', 'fsdp')), may hold values from 0.05 to 1
- gate_weight: bfloat16 [64, 4096, 1024], P('ep', None, 'fsdp'), may hold values from -0.09375 to 0.09375
- up_weight: bfloat16 [64, 4096, 1024], P('ep', None, 'fsdp'), may hold values from -0.09375 to 0.09375
- down_weight: bfloat16 [64, 4096, 1024], P('ep', None, 'fsdp'), may hold values from -0.1875 to 0.1875
Outputs:
- mixed: bfloat16 [12288, 4096], P(('ep', 'fsdp'))
Inputs may be any that keep to these rules, and one draw needn't show every extreme that they name: `expert_ids`: each row names 8 different experts. Among the rows of one device's aligned block of 48 tokens no expert is named more than 9 times, and in some blocks one expert is named exactly 9 times.
All inputs are finite; a program needn't handle non-finite values.
Results may differ from a plain program's by a relative error of at most 0.0057.
Values may be sent and summed in bfloat16 or wider, within the bound.
No kernel may reach another device: no remote copies, remote signals or barrier semaphores. Data moves between devices by JAX's collectives and lax.ppermute only.
A program may use at most 128 MiB of HBM per device.

v0:
```python
import jax
import jax.numpy as jnp
from jax import lax
from jax.experimental.layout import Layout, with_layout_constraint
from jax.sharding import Mesh, PartitionSpec as P

NYL, NZ, NX, NYH, NC = 2, 8, 4, 2, 2
AXES = ("yl", "z", "x", "yh", "core")
CAP = 9
EXTRA = 128
OUT = (1792, 2304)
UP = 1024
LOOPED = (True, True)


def plane_groups():
    def index(yl, z, x, yh, core):
        return (((yl * NZ + z) * NX + x) * NYH + yh) * NC + core

    groups = []
    for z in range(NZ):
        for core in range(NC):
            for half in range(NYH):
                groups.append(
                    [index(yl, z, x, half ^ (yl if core else 0), core) for yl in range(NYL) for x in range(NX)]
                )
    return groups


def exchange(block):
    return lax.all_to_all(
        block, AXES, 0, 0, axis_index_groups=plane_groups(), tiled=True
    )


def swap(block, axis):
    return lax.ppermute(block, axis, [(0, 1), (1, 0)])


def along_z(block, step):
    return lax.ppermute(block, "z", [(i, (i + step) % NZ) for i in range(NZ)])


def parts_of(value, count):
    parts = []
    for _ in range(count):
        part = value.astype(jnp.bfloat16)
        value = value - part.astype(jnp.float32)
        parts.append(part)
    return parts


def summed(blocks, looped):
    middle = NZ // 2

    def turn(hop, state):
        down, up = state
        down = along_z(down.astype(jnp.bfloat16), -1)
        up = along_z(up.astype(jnp.bfloat16), 1)
        down = down.astype(jnp.float32) + blocks[1 + hop].astype(jnp.float32)
        up = up.astype(jnp.float32) + blocks[NZ - 2 - hop].astype(jnp.float32)
        return down, up

    state = blocks[0].astype(jnp.float32), blocks[NZ - 1].astype(jnp.float32)
    if looped:
        state = lax.fori_loop(0, middle - 1, turn, state)
    else:
        for hop in range(middle - 1):
            state = turn(hop, state)
    down, up = state
    down = along_z(down.astype(jnp.bfloat16), -1)
    return (down.astype(jnp.float32) + up).astype(jnp.bfloat16)


def local(tokens, expert_ids, gate_values, gate_weight, up_weight, down_weight):
    rows, width = tokens.shape
    top = expert_ids.shape[1]
    dests = NYL * NX
    cap = CAP * NZ

    own_gate, own_up, own_down = gate_weight[0], up_weight[0], down_weight[0]
    near_gate, near_up, near_down = swap(own_gate, "core"), swap(own_up, "core"), swap(own_down, "core")

    def pieces(own, near, start, size):
        own = own[start : start + size]
        far = swap(own, "yh")
        hop = swap(far, "core")
        return jnp.concatenate([own, near[start : start + size], far, hop], axis=1)

    gate = pieces(own_gate, near_gate, 0, width)
    up0 = pieces(own_up, near_up, 0, UP)
    up1 = pieces(own_up, near_up, UP, width - UP)
    downs = [pieces(own_down, near_down, 0, OUT[0]), pieces(own_down, near_down, OUT[0], OUT[1])]

    notes = jnp.concatenate([expert_ids.astype(jnp.bfloat16)] + parts_of(gate_values, 2), axis=1)
    notes = jnp.pad(notes, ((0, 0), (0, EXTRA - notes.shape[1])))
    own = jnp.concatenate([notes, tokens], axis=1)
    whole = jnp.broadcast_to(own[None], (NZ,) + own.shape).reshape(NZ * rows, own.shape[1])

    def turn(hop, state):
        whole, ahead, behind = state
        ahead = along_z(ahead, 1)
        behind = along_z(behind, -1)
        whole = lax.dynamic_update_slice(whole, ahead, ((NZ // 2 - 1 - hop) * rows, 0))
        whole = lax.dynamic_update_slice(whole, behind, ((NZ // 2 + 1 + hop) * rows, 0))
        return whole, ahead, behind

    whole, ahead, _ = lax.fori_loop(0, NZ // 2 - 1, turn, (whole, own, own))
    ahead = along_z(ahead, 1)
    whole = lax.dynamic_update_slice(whole, ahead, (0, 0))
    whole = with_layout_constraint(whole, Layout(major_to_minor=(0, 1)))

    count = NZ * rows
    notes = whole[:, : 3 * top].astype(jnp.float32)
    ids = notes[:, :top].astype(jnp.int32)
    values = notes[:, top : 2 * top] + notes[:, 2 * top :]
    dest = jnp.arange(dests, dtype=jnp.int32)
    expert = (dest // NX) * (NZ * NX) + lax.axis_index("z") * NX + dest % NX
    hit = ids[:, :, None] == expert[None, None, :]
    named = jnp.any(hit, axis=1)
    weight = jnp.sum(jnp.where(hit, values[:, :, None], 0.0), axis=1)
    order = jnp.arange(count, dtype=jnp.int32)
    before = (order[None, :] < order[:, None]).astype(jnp.bfloat16)
    rank = jnp.dot(before, named.astype(jnp.bfloat16), preferred_element_type=jnp.float32).astype(jnp.int32)
    slot = jnp.where(named, rank + cap * dest[None, :], -1)
    slots = jnp.arange(dests * cap, dtype=jnp.int32)

    def placed(slot):
        return (jnp.repeat(slot, cap, axis=1) == slots[None, :]).astype(jnp.bfloat16)

    pack = placed(slot)

    weights = jnp.pad(jnp.concatenate(parts_of(weight, 2), axis=1), ((0, 0), (0, EXTRA - 2 * dests)))
    whole = lax.dynamic_update_slice(whole, weights, (0, 0))
    packed = lax.dot_general(pack, whole, (((0,), (0,)), ((), ())), preferred_element_type=jnp.float32)
    packed = packed.astype(jnp.bfloat16).reshape(dests, cap, EXTRA + width)
    arrived = exchange(packed).reshape(dests * cap, EXTRA + width)
    mine = lax.axis_index("yl") * NX + lax.axis_index("x")
    weight = arrived[:, : 2 * dests].astype(jnp.float32)
    weight = jnp.where(jnp.arange(2 * dests) % dests == mine, weight, 0.0)
    weight = jnp.sum(weight, axis=1, keepdims=True)
    arrived = arrived[:, EXTRA:]

    gate_part = jnp.dot(arrived, gate, preferred_element_type=jnp.float32)
    up_part = jnp.dot(arrived[:, :UP], up0, preferred_element_type=jnp.float32)
    up_part = jnp.dot(arrived[:, UP:], up1, preferred_element_type=jnp.float32) + up_part
    hidden = (jax.nn.silu(gate_part) * up_part).astype(jnp.bfloat16)

    mixed = []
    for c, size in enumerate(OUT):
        out = lax.dot_general(hidden, downs[c], (((1,), (1,)), ((), ())), preferred_element_type=jnp.float32)
        out = (out * weight).astype(jnp.bfloat16).reshape(dests, cap, size)
        out = exchange(out).reshape(dests * cap, size)
        both = jnp.dot(pack, out, preferred_element_type=jnp.float32)
        both = both.astype(jnp.bfloat16).reshape(NZ, rows, size)
        mixed.append(summed(both, looped=LOOPED[c]))
    return jnp.concatenate(mixed, axis=1)


def solution(mesh):
    fine = Mesh(mesh.devices.reshape(NYL, NZ, NX, NYH, NC), AXES)
    rows = P(AXES, None)
    weights = P(("yl", "z", "x"), None, ("yh", "core"))
    return jax.shard_map(
        local,
        mesh=fine,
        in_specs=(rows, rows, rows, weights, weights, weights),
        out_specs=rows,
        check_vma=False,
    )
```

profile of v0, /device:TPU:14, one launch (start us, length us, event | category | flops | bytes accessed | tf_op | source)
XLA Modules:
  0.0 372.6 jit_solution(7218983944710911625)
XLA Ops:
  1.6 1.0 fusion.59
  2.6 1.9 broadcast_in_dim.41
  4.5 42.9 %while.51 = (s32[]{:T(128)}, bf16[384,4224]{1,0:T(8,128)(2,1)}, bf16[48,4224]{1,0:T(8,128)(2,1)S(1)}, bf16[48,4224]{1,0:T(8,128)(2,1)S(1)}, s32[]{:T(128)}, /*in...) while((s32[]{:T(128)}, bf16[384,4224]{1,0:T(8,128)(2,1)}, bf16[48,4224]{1,0:T(8,128)(2,1)S(1)}, ...), condition=%wide.region_1.2_spmd, body=%wide.region_0.1_spmd.sunk | while | flops 12 | bytes 6488369 | solution.py:108
  4.5 1.9 collective-permute-start
  6.4 3.9 %collective-permute-start.1 = (bf16[48,4224]{1,0:T(8,128)(2,1)S(1)}, bf16[48,4224]{1,0:T(8,128)(2,1)S(1)}, u32[]{:S(2)}, u32[]{:S(2)}) collective-permute-start(bf16[48,4224]{1,0:T(8,128)(2,1)S(1)} %get-tuple-element.437), channel_id=1, source_target_pairs={{0,112},{16,0},{32,16},{48,32},{64,48},{80,64},{96,80},{112,96},{1... | collective-permute-start | bytes 1216520 | tf_op jit(solution)/shard_map/while/body/eval_jaxpr/ppermute | solution.py:41
  10.4 9.4 %collective-permute-done = bf16[48,4224]{1,0:T(8,128)(2,1)S(1)} collective-permute-done((bf16[48,4224]{1,0:T(8,128)(2,1)S(1)}, bf16[48,4224]{1,0:T(8,128)(2,1)S(1)}, u32[]{:S(2)}, u32[]{:S(2)}) %collective-permute-start) | collective-permute-done | bytes 405536 | tf_op jit(solution)/shard_map/while/body/eval_jaxpr/ppermute | solution.py:41
  21.4 3.2 collective-permute-start.1
  24.7 8.5 %collective-permute-done = bf16[48,4224]{1,0:T(8,128)(2,1)S(1)} collective-permute-done((bf16[48,4224]{1,0:T(8,128)(2,1)S(1)}, bf16[48,4224]{1,0:T(8,128)(2,1)S(1)}, u32[]{:S(2)}, u32[]{:S(2)}) %collective-permute-start) | collective-permute-done | bytes 405536 | tf_op jit(solution)/shard_map/while/body/eval_jaxpr/ppermute | solution.py:41
  34.9 1.8 collective-permute-start
  36.7 1.4 collective-permute-start.1
  38.1 7.7 %collective-permute-done = bf16[48,4224]{1,0:T(8,128)(2,1)S(1)} collective-permute-done((bf16[48,4224]{1,0:T(8,128)(2,1)S(1)}, bf16[48,4224]{1,0:T(8,128)(2,1)S(1)}, u32[]{:S(2)}, u32[]{:S(2)}) %collective-permute-start) | collective-permute-done | bytes 405536 | tf_op jit(solution)/shard_map/while/body/eval_jaxpr/ppermute | solution.py:41
  47.4 1.5 collective-permute-start.6
  48.9 8.5 %collective-permute-done.6 = bf16[48,4224]{1,0:T(8,128)(2,1)S(1)} collective-permute-done((bf16[48,4224]{1,0:T(8,128)(2,1)S(1)}, bf16[48,4224]{1,0:T(8,128)(2,1)S(1)}, u32[]{:S(2)}, u32[]{:S(2)}) %collective-permute-start.6) | collective-permute-done | bytes 405536 | tf_op jit(solution)/shard_map/ppermute | solution.py:41
  58.2 0.9 slice_convert_fusion.5
  60.8 6.3 %convolution_convert_fusion = bf16[576,4224]{1,0:T(8,128)(2,1)} fusion(pred[384,576]{0,1:T(32,128)(4,1)S(1)} %bitcast_compare_fusion, bf16[384,4224]{1,0:T(8,128)(2,1)} %pad_dynamic-update-slice_fusion), kind=kOutput, calls=%fused_computation.14 | convolution fusion | flops 1870995456 | bytes 8331264 | tf_op jit(solution)/shard_map/dot_general | solution.py:135
  67.2 5.8 %all-to-all-start = ((bf16[8,72,4224]{2,1,0:T(8,128)(2,1)}), bf16[8,72,4224]{2,1,0:T(8,128)(2,1)}, u32[]{:S(2)}, u32[]{:S(2)}) async-start(bf16[8,72,4224]{2,1,0:T(8,128)(2,1)} %bitcast.55), calls=%async_computation | async-start | bytes 9732096 | tf_op jit(solution)/shard_map/all_to_all | solution.py:31
  73.0 2.3 collective-permute-start.8
  76.1 1.2 collective-permute-start.13
  77.6 85.0 %collective-permute-done.13 = bf16[1024,256]{1,0:T(8,128)(2,1)S(1)} collective-permute-done((bf16[1024,256]{1,0:T(8,128)(2,1)S(1)}, bf16[1024,256]{1,0:T(8,128)(2,1)S(1)}, u32[]{:S(2)}, u32[]{:S(2)}) %collective-permute-start.13) | collective-permute-done | bytes 524320 | tf_op jit(solution)/shard_map/ppermute | solution.py:37
  162.6 1.4 slice_bitcast_fusion
  164.5 1.4 collective-permute-start.11
  166.1 2.2 collective-permute-start.19
  168.4 1.5 collective-permute-start.16
  169.9 2.2 slice.111
  172.1 2.9 fusion.37
  175.1 28.5 %collective-permute-done.11 = bf16[3072,256]{1,0:T(8,128)(2,1)} collective-permute-done((bf16[3072,256]{1,0:T(8,128)(2,1)}, bf16[3072,256]{1,0:T(8,128)(2,1)}, u32[]{:S(2)}, u32[]{:S(2)}) %collective-permute-start.11) | collective-permute-done | bytes 1572896 | tf_op jit(solution)/shard_map/ppermute | solution.py:37
  203.6 1.1 select_reduce_fusion
  204.6 43.0 %collective-permute-done.16 = bf16[1792,256]{1,0:T(8,128)(2,1)} collective-permute-done((bf16[1792,256]{1,0:T(8,128)(2,1)S(1)}, bf16[1792,256]{1,0:T(8,128)(2,1)}, u32[]{:S(2)}, u32[]{:S(2)}) %collective-permute-start.16) | collective-permute-done | bytes 917536 | tf_op jit(solution)/shard_map/ppermute | solution.py:37
  248.2 9.2 %fusion = f32[576,1024]{1,0:T(8,128)S(1)} fusion(bf16[4096,256]{1,0:T(8,128)(2,1)} %collective-permute-done.9, bf16[4096,256]{1,0:T(8,128)(2,1)} %collective-permute-done.8, bf16[4096,256]{1,0:T(8,128)(2,1)} %collective-permute-done.7, bf16[4096,256]{1,0:T(8,128)(2,1)} %bitcast.8, bf16[576,4224]{1,0:T(8,128)(2,1)} %bitcast.7), kind=kOutput, calls=%fused_computation.6 | convolution fusion | flops 4865392640 | bytes 15466496 | tf_op jit(solution)/shard_map/dot_general | solution.py:144
  257.4 7.1 %multiply_convert_fusion.2 = bf16[576,1024]{1,0:T(8,128)(2,1)S(1)} fusion(f32[576,1024]{1,0:T(8,128)S(1)} %fusion.37, f32[576,1024]{1,0:T(8,128)S(1)} %fusion, bf16[3072,256]{1,0:T(8,128)(2,1)S(1)} %collective-permute-done.12, bf16[3072,256]{1,0:T(8,128)(2,1)} %collective-permute-done.11, bf16[3072,256]{1,0:T(8,128)(2,1)S(1)} %slice-done.1, ...), kind=kOutput, calls=%fused_computation.46 | convolution fusion | flops 3653173248 | bytes 15728640 | tf_op jit(solution)/shard_map/dot_general | solution.py:146
  264.6 5.3 %multiply_convert_fusion.1 = bf16[576,1792]{1,0:T(8,128)(2,1)} fusion(bf16[576,1024]{1,0:T(8,128)(2,1)S(1)} %multiply_convert_fusion.2, bf16[1792,256]{1,0:T(8,128)(2,1)S(1)} %collective-permute-done.17, bf16[1792,256]{1,0:T(8,128)(2,1)} %collective-permute-done.16, bf16[1792,256]{1,0:T(8,128)(2,1)S(1)} %copy-done.4, ...), kind=kOutput, calls=%fused_computation.34 | convolution fusion | flops 2130673664 | bytes 6916352 | tf_op jit(solution)/shard_map/dot_general | solution.py:151
  269.9 5.4 %all-to-all-start.1 = ((bf16[8,72,1792]{2,1,0:T(8,128)(2,1)}), bf16[8,72,1792]{2,1,0:T(8,128)(2,1)S(1)}, u32[]{:S(2)}, u32[]{:S(2)}) async-start(bf16[8,72,1792]{2,1,0:T(8,128)(2,1)} %bitcast.61), calls=%async_computation.1 | async-start | bytes 4128768 | tf_op jit(solution)/shard_map/all_to_all | solution.py:31
  275.3 1.3 slice.115
  276.7 6.3 %multiply_convert_fusion = bf16[576,2304]{1,0:T(8,128)(2,1)} fusion(bf16[576,1024]{1,0:T(8,128)(2,1)} %copy-done.9, bf16[2304,256]{1,0:T(8,128)(2,1)} %collective-permute-done.20, bf16[2304,256]{1,0:T(8,128)(2,1)} %collective-permute-done.19, bf16[2304,256]{1,0:T(8,128)(2,1)S(1)} %slice.115, bf16[2304,256]{1,0:T(8,128)(2,1)S(1)} %slice_bitcast_fusion.1, ...), kind=kOutput, calls=%fused_computation.23 | convolution fusion | flops 2739437568 | bytes 8554752 | tf_op jit(solution)/shard_map/dot_general | solution.py:151
  283.0 16.4 %all-to-all-done.1 = bf16[8,72,1792]{2,1,0:T(8,128)(2,1)S(1)} async-done(((bf16[8,72,1792]{2,1,0:T(8,128)(2,1)}), bf16[8,72,1792]{2,1,0:T(8,128)(2,1)S(1)}, u32[]{:S(2)}, u32[]{:S(2)}) %all-to-all-start.1) | async-done | bytes 2064416 | tf_op jit(solution)/shard_map/all_to_all | solution.py:31
  299.4 1.3 copy-done.3
  300.7 7.0 %all-to-all-start.2 = ((bf16[8,72,2304]{2,1,0:T(8,128)(2,1)}), bf16[8,72,2304]{2,1,0:T(8,128)(2,1)}, u32[]{:S(2)}, u32[]{:S(2)}) async-start(bf16[8,72,2304]{2,1,0:T(8,128)(2,1)} %bitcast.18), calls=%async_computation.2 | async-start | bytes 5308416 | tf_op jit(solution)/shard_map/all_to_all | solution.py:31
  307.7 2.9 fusion.34
  311.3 24.1 %while.52 = (s32[]{:T(128)}, bf16[48,1792]{1,0:T(8,128)(2,1)}, f32[48,1792]{1,0:T(8,128)S(1)}, bf16[8,48,1792]{2,1,0:T(8,128)(2,1)S(1)}, s32[]{:T(128)}, /*index=5*/s32[]{:T(128)}, s32[]{:T(128)}, s32[]{:T(128)}, s32[]{:T(128)}) while((s32[]{:T(128)}, bf16[48,1792]{1,0:T(8,128)(2,1)}, f32[48,1792]{1,0:T(8,128)S(1)}, ...), condition=%wide.region_6.7_spmd, body=%wide.region_5.6_spmd.sunk | while | flops 688137 | bytes 3096845 | solution.py:66
  311.3 1.6 collective-permute-start.2
  313.5 3.8 %collective-permute-done.2 = bf16[48,1792]{1,0:T(8,128)(2,1)S(1)} collective-permute-done((bf16[48,1792]{1,0:T(8,128)(2,1)}, bf16[48,1792]{1,0:T(8,128)(2,1)S(1)}, u32[]{:S(2)}, u32[]{:S(2)}) %collective-permute-start.2) | collective-permute-done | bytes 172064 | tf_op jit(solution)/shard_map/while/body/eval_jaxpr/ppermute | solution.py:41
  318.0 1.8 collective-permute-done.3
  319.8 1.2 collective-permute-start.2
  321.0 1.0 collective-permute-start.3
  322.0 3.5 collective-permute-done.2
  326.2 1.5 collective-permute-done.3
  327.8 0.9 collective-permute-start.2
  328.7 1.3 collective-permute-start.3
  330.0 3.5 collective-permute-done.2
  334.2 1.2 collective-permute-done.3
  335.4 0.9 collective-permute-start.18
  336.3 1.9 all-to-all-done.2
  338.2 3.4 fusion.24
  341.7 24.1 %while.53 = (s32[]{:T(128)}, bf16[48,2304]{1,0:T(8,128)(2,1)S(1)}, f32[48,2304]{1,0:T(8,128)S(1)}, bf16[8,48,2304]{2,1,0:T(8,128)(2,1)S(1)}, s32[]{:T(128)}, /*index=5*/s32[]{:T(128)}, s32[]{:T(128)}, s32[]{:T(128)}, s32[]{:T(128)}) while((s32[]{:T(128)}, bf16[48,2304]{1,0:T(8,128)(2,1)S(1)}, f32[48,2304]{1,0:T(8,128)S(1)}, ...), condition=%wide.region_8.9_spmd, body=%wide.region_7.8_spmd.sunk | while | flops 884745 | bytes 3981581 | solution.py:66
  341.7 1.7 collective-permute-start.4
  343.9 4.1 %collective-permute-done.4 = bf16[48,2304]{1,0:T(8,128)(2,1)S(1)} collective-permute-done((bf16[48,2304]{1,0:T(8,128)(2,1)S(1)}, bf16[48,2304]{1,0:T(8,128)(2,1)S(1)}, u32[]{:S(2)}, u32[]{:S(2)}) %collective-permute-start.4) | collective-permute-done | bytes 221216 | tf_op jit(solution)/shard_map/while/body/eval_jaxpr/ppermute | solution.py:41
  348.0 2.6 collective-permute-done.5
  351.0 1.9 collective-permute-start.5
  352.9 3.8 %collective-permute-done.4 = bf16[48,2304]{1,0:T(8,128)(2,1)S(1)} collective-permute-done((bf16[48,2304]{1,0:T(8,128)(2,1)S(1)}, bf16[48,2304]{1,0:T(8,128)(2,1)S(1)}, u32[]{:S(2)}, u32[]{:S(2)}) %collective-permute-start.4) | collective-permute-done | bytes 221216 | tf_op jit(solution)/shard_map/while/body/eval_jaxpr/ppermute | solution.py:41
  356.8 1.5 collective-permute-done.5
  358.5 2.1 collective-permute-start.5
  360.5 4.3 %collective-permute-done.4 = bf16[48,2304]{1,0:T(8,128)(2,1)S(1)} collective-permute-done((bf16[48,2304]{1,0:T(8,128)(2,1)S(1)}, bf16[48,2304]{1,0:T(8,128)(2,1)S(1)}, u32[]{:S(2)}, u32[]{:S(2)}) %collective-permute-start.4) | collective-permute-done | bytes 221216 | tf_op jit(solution)/shard_map/while/body/eval_jaxpr/ppermute | solution.py:41
  366.5 0.9 add_convert_fusion.1
  367.4 4.3 %collective-permute-done.21 = bf16[48,2304]{1,0:T(8,128)(2,1)S(1)} collective-permute-done((bf16[48,2304]{1,0:T(8,128)(2,1)S(1)}, bf16[48,2304]{1,0:T(8,128)(2,1)S(1)}, u32[]{:S(2)}, u32[]{:S(2)}) %collective-permute-start.21) | collective-permute-done | bytes 221216 | tf_op jit(solution)/shard_map/ppermute | solution.py:41
  (111 shorter events, 18.5 us)
Async XLA Ops:
  4.5 15.2 %collective-permute-start = (bf16[48,4224]{1,0:T(8,128)(2,1)S(1)}, bf16[48,4224]{1,0:T(8,128)(2,1)S(1)}, u32[]{:S(2)}, u32[]{:S(2)}) collective-permute-start(bf16[48,4224]{1,0:T(8,128)(2,1)S(1)} %get-tuple-element.436), channel_id=1, source_target_pairs={{0,16},{16,32},{32,48},{48,64},{64,80},{80,96},{96,112},{112,0},{1... | collective-permute-start | bytes 1216520 | tf_op jit(solution)/shard_map/while/body/eval_jaxpr/ppermute | solution.py:41
  6.4 13.3 %collective-permute-start.1 = (bf16[48,4224]{1,0:T(8,128)(2,1)S(1)}, bf16[48,4224]{1,0:T(8,128)(2,1)S(1)}, u32[]{:S(2)}, u32[]{:S(2)}) collective-permute-start(bf16[48,4224]{1,0:T(8,128)(2,1)S(1)} %get-tuple-element.437), channel_id=1, source_target_pairs={{0,112},{16,0},{32,16},{48,32},{64,48},{80,64},{96,80},{112,96},{1... | collective-permute-start | bytes 1216520 | tf_op jit(solution)/shard_map/while/body/eval_jaxpr/ppermute | solution.py:41
  21.4 11.8 %collective-permute-start = (bf16[48,4224]{1,0:T(8,128)(2,1)S(1)}, bf16[48,4224]{1,0:T(8,128)(2,1)S(1)}, u32[]{:S(2)}, u32[]{:S(2)}) collective-permute-start(bf16[48,4224]{1,0:T(8,128)(2,1)S(1)} %get-tuple-element.436), channel_id=1, source_target_pairs={{0,16},{16,32},{32,48},{48,64},{64,80},{80,96},{96,112},{112,0},{1... | collective-permute-start | bytes 1216520 | tf_op jit(solution)/shard_map/while/body/eval_jaxpr/ppermute | solution.py:41
  21.4 11.8 %collective-permute-start.1 = (bf16[48,4224]{1,0:T(8,128)(2,1)S(1)}, bf16[48,4224]{1,0:T(8,128)(2,1)S(1)}, u32[]{:S(2)}, u32[]{:S(2)}) collective-permute-start(bf16[48,4224]{1,0:T(8,128)(2,1)S(1)} %get-tuple-element.437), channel_id=1, source_target_pairs={{0,112},{16,0},{32,16},{48,32},{64,48},{80,64},{96,80},{112,96},{1... | collective-permute-start | bytes 1216520 | tf_op jit(solution)/shard_map/while/body/eval_jaxpr/ppermute | solution.py:41
  34.9 10.9 %collective-permute-start = (bf16[48,4224]{1,0:T(8,128)(2,1)S(1)}, bf16[48,4224]{1,0:T(8,128)(2,1)S(1)}, u32[]{:S(2)}, u32[]{:S(2)}) collective-permute-start(bf16[48,4224]{1,0:T(8,128)(2,1)S(1)} %get-tuple-element.436), channel_id=1, source_target_pairs={{0,16},{16,32},{32,48},{48,64},{64,80},{80,96},{96,112},{112,0},{1... | collective-permute-start | bytes 1216520 | tf_op jit(solution)/shard_map/while/body/eval_jaxpr/ppermute | solution.py:41
  36.7 9.1 %collective-permute-start.1 = (bf16[48,4224]{1,0:T(8,128)(2,1)S(1)}, bf16[48,4224]{1,0:T(8,128)(2,1)S(1)}, u32[]{:S(2)}, u32[]{:S(2)}) collective-permute-start(bf16[48,4224]{1,0:T(8,128)(2,1)S(1)} %get-tuple-element.437), channel_id=1, source_target_pairs={{0,112},{16,0},{32,16},{48,32},{64,48},{80,64},{96,80},{112,96},{1... | collective-permute-start | bytes 1216520 | tf_op jit(solution)/shard_map/while/body/eval_jaxpr/ppermute | solution.py:41
  47.4 10.0 %collective-permute-start.6 = (bf16[48,4224]{1,0:T(8,128)(2,1)S(1)}, bf16[48,4224]{1,0:T(8,128)(2,1)S(1)}, u32[]{:S(2)}, u32[]{:S(2)}) collective-permute-start(bf16[48,4224]{1,0:T(8,128)(2,1)S(1)} %get-tuple-element.310), channel_id=1, source_target_pairs={{0,16},{16,32},{32,48},{48,64},{64,80},{80,96},{96,112},{112,0},{1... | collective-permute-start | bytes 1216520 | tf_op jit(solution)/shard_map/ppermute | solution.py:41
  67.2 8.1 %copy-start = (bf16[1,4096,256]{2,1,0:T(8,128)(2,1)S(1)}, bf16[1,4096,256]{2,1,0:T(8,128)(2,1)}, u32[]{:S(2)}) copy-start(bf16[1,4096,256]{2,1,0:T(8,128)(2,1)} %param.16) | copy-start | bytes 6291460
  67.2 104.9 %all-to-all-start = ((bf16[8,72,4224]{2,1,0:T(8,128)(2,1)}), bf16[8,72,4224]{2,1,0:T(8,128)(2,1)}, u32[]{:S(2)}, u32[]{:S(2)}) async-start(bf16[8,72,4224]{2,1,0:T(8,128)(2,1)} %bitcast.55), calls=%async_computation | async-start | bytes 9732096 | tf_op jit(solution)/shard_map/all_to_all | solution.py:31
  73.0 93.0 %copy-start.1 = (bf16[1,4096,256]{2,1,0:T(8,128)(2,1)S(1)}, bf16[1,4096,256]{2,1,0:T(8,128)(2,1)}, u32[]{:S(2)}) copy-start(bf16[1,4096,256]{2,1,0:T(8,128)(2,1)} %param.17) | copy-start | bytes 6291460
  73.0 92.9 %collective-permute-start.8 = (bf16[4096,256]{1,0:T(8,128)(2,1)}, bf16[4096,256]{1,0:T(8,128)(2,1)}, u32[]{:S(2)}, u32[]{:S(2)}) collective-permute-start(bf16[4096,256]{1,0:T(8,128)(2,1)} %bitcast.8), channel_id=1, source_target_pairs={{0,2},{2,0},{1,3},{3,1},{4,6},{6,4},{5,7},{7,5},{8,10},{10,8},{9,1... | collective-permute-start | bytes 6291464 | tf_op jit(solution)/shard_map/ppermute | solution.py:37
  75.3 90.8 %collective-permute-start.10 = (bf16[4096,256]{1,0:T(8,128)(2,1)S(1)}, bf16[4096,256]{1,0:T(8,128)(2,1)S(1)}, u32[]{:S(2)}, u32[]{:S(2)}) collective-permute-start(bf16[4096,256]{1,0:T(8,128)(2,1)S(1)} %bitcast.59), channel_id=1, source_target_pairs={{0,1},{1,0},{2,3},{3,2},{4,5},{5,4},{6,7},{7,6},{8,9},{9,8},{10,11... | collective-permute-start | bytes 6291464 | tf_op jit(solution)/shard_map/ppermute | solution.py:37
  75.3 0.8 copy-start.5
  76.1 86.4 %collective-permute-start.13 = (bf16[1024,256]{1,0:T(8,128)(2,1)S(1)}, bf16[1024,256]{1,0:T(8,128)(2,1)S(1)}, u32[]{:S(2)}, u32[]{:S(2)}) collective-permute-start(bf16[1024,256]{1,0:T(8,128)(2,1)S(1)} %slice_bitcast_fusion.3), channel_id=1, source_target_pairs={{0,2},{2,0},{1,3},{3,1},{4,6},{6,4},{5,7},{7,5},{8,10},{10,8},{9,1... | collective-permute-start | bytes 1572872 | tf_op jit(solution)/shard_map/ppermute | solution.py:37
  77.4 91.0 %collective-permute-start.15 = (bf16[4096,256]{1,0:T(8,128)(2,1)}, bf16[4096,256]{1,0:T(8,128)(2,1)}, u32[]{:S(2)}, u32[]{:S(2)}) collective-permute-start(bf16[4096,256]{1,0:T(8,128)(2,1)} %bitcast.60), channel_id=1, source_target_pairs={{0,1},{1,0},{2,3},{3,2},{4,5},{5,4},{6,7},{7,6},{8,9},{9,8},{10,11... | collective-permute-start | bytes 6291464 | tf_op jit(solution)/shard_map/ppermute | solution.py:37
  162.6 3.3 copy-start.7
  162.6 1.9 collective-permute-start.14
  163.9 84.3 %collective-permute-start.7 = (bf16[4096,256]{1,0:T(8,128)(2,1)}, bf16[4096,256]{1,0:T(8,128)(2,1)}, u32[]{:S(2)}, u32[]{:S(2)}) collective-permute-start(bf16[4096,256]{1,0:T(8,128)(2,1)} %bitcast.8), channel_id=1, source_target_pairs={{0,1},{1,0},{2,3},{3,2},{4,5},{5,4},{6,7},{7,6},{8,9},{9,8},{10,11... | collective-permute-start | bytes 6291464 | tf_op jit(solution)/shard_map/ppermute | solution.py:37
  164.5 1.4 copy-start.8
  164.5 39.1 %collective-permute-start.11 = (bf16[3072,256]{1,0:T(8,128)(2,1)}, bf16[3072,256]{1,0:T(8,128)(2,1)}, u32[]{:S(2)}, u32[]{:S(2)}) collective-permute-start(bf16[3072,256]{1,0:T(8,128)(2,1)} %slice_bitcast_fusion), channel_id=1, source_target_pairs={{0,2},{2,0},{1,3},{3,1},{4,6},{6,4},{5,7},{7,5},{8,10},{10,8},{9,1... | collective-permute-start | bytes 4718600 | tf_op jit(solution)/shard_map/ppermute | solution.py:37
  165.9 82.3 %collective-permute-start.9 = (bf16[4096,256]{1,0:T(8,128)(2,1)}, bf16[4096,256]{1,0:T(8,128)(2,1)}, u32[]{:S(2)}, u32[]{:S(2)}) collective-permute-start(bf16[4096,256]{1,0:T(8,128)(2,1)} %collective-permute-done.8), channel_id=1, source_target_pairs={{0,1},{1,0},{2,3},{3,2},{4,5},{5,4},{6,7},{7,6},{8,9},{9,8},{10,11... | collective-permute-start | bytes 6291464 | tf_op jit(solution)/shard_map/ppermute | solution.py:37
  166.1 2.3 copy-start.2
  166.1 81.6 %collective-permute-start.19 = (bf16[2304,256]{1,0:T(8,128)(2,1)S(1)}, bf16[2304,256]{1,0:T(8,128)(2,1)}, u32[]{:S(2)}, u32[]{:S(2)}) collective-permute-start(bf16[2304,256]{1,0:T(8,128)(2,1)S(1)} %slice_bitcast_fusion.1), channel_id=1, source_target_pairs={{0,2},{2,0},{1,3},{3,1},{4,6},{6,4},{5,7},{7,5},{8,10},{10,8},{9,1... | collective-permute-start | bytes 3538952 | tf_op jit(solution)/shard_map/ppermute | solution.py:37
  168.4 3.7 copy-start.6
  168.4 3.7 slice-start
  168.4 79.2 %collective-permute-start.16 = (bf16[1792,256]{1,0:T(8,128)(2,1)S(1)}, bf16[1792,256]{1,0:T(8,128)(2,1)}, u32[]{:S(2)}, u32[]{:S(2)}) collective-permute-start(bf16[1792,256]{1,0:T(8,128)(2,1)S(1)} %slice_bitcast_fusion.2), channel_id=1, source_target_pairs={{0,2},{2,0},{1,3},{3,1},{4,6},{6,4},{5,7},{7,5},{8,10},{10,8},{9,1... | collective-permute-start | bytes 2752520 | tf_op jit(solution)/shard_map/ppermute | solution.py:37
  203.6 53.8 %collective-permute-start.12 = (bf16[3072,256]{1,0:T(8,128)(2,1)}, bf16[3072,256]{1,0:T(8,128)(2,1)S(1)}, u32[]{:S(2)}, u32[]{:S(2)}) collective-permute-start(bf16[3072,256]{1,0:T(8,128)(2,1)} %collective-permute-done.11), channel_id=1, source_target_pairs={{0,1},{1,0},{2,3},{3,2},{4,5},{5,4},{6,7},{7,6},{8,9},{9,8},{10,11... | collective-permute-start | bytes 4718600 | tf_op jit(solution)/shard_map/ppermute | solution.py:37
  204.6 52.8 %slice-start.1 = ((bf16[4096,256]{1,0:T(8,128)(2,1)}), bf16[3072,256]{1,0:T(8,128)(2,1)S(1)}, s32[]{:S(2)}) async-start(bf16[4096,256]{1,0:T(8,128)(2,1)} %copy-done.2), calls=%async_computation.4 | async-start | bytes 3145728 | tf_op jit(solution)/shard_map/slice | solution.py:88
  247.7 16.9 %collective-permute-start.17 = (bf16[1792,256]{1,0:T(8,128)(2,1)}, bf16[1792,256]{1,0:T(8,128)(2,1)S(1)}, u32[]{:S(2)}, u32[]{:S(2)}) collective-permute-start(bf16[1792,256]{1,0:T(8,128)(2,1)} %collective-permute-done.16), channel_id=1, source_target_pairs={{0,1},{1,0},{2,3},{3,2},{4,5},{5,4},{6,7},{7,6},{8,9},{9,8},{10,11... | collective-permute-start | bytes 2752520 | tf_op jit(solution)/shard_map/ppermute | solution.py:37
  247.7 29.0 %collective-permute-start.20 = (bf16[2304,256]{1,0:T(8,128)(2,1)}, bf16[2304,256]{1,0:T(8,128)(2,1)}, u32[]{:S(2)}, u32[]{:S(2)}) collective-permute-start(bf16[2304,256]{1,0:T(8,128)(2,1)} %collective-permute-done.19), channel_id=1, source_target_pairs={{0,1},{1,0},{2,3},{3,2},{4,5},{5,4},{6,7},{7,6},{8,9},{9,8},{10,11... | collective-permute-start | bytes 3538952 | tf_op jit(solution)/shard_map/ppermute | solution.py:37
  257.4 7.2 %copy-start.4 = (bf16[1792,256]{1,0:T(8,128)(2,1)S(1)}, bf16[1792,256]{1,0:T(8,128)(2,1)}, u32[]{:S(2)}) copy-start(bf16[1792,256]{1,0:T(8,128)(2,1)} %slice.111) | copy-start | bytes 2752516
  264.6 5.3 %copy-start.9 = (bf16[576,1024]{1,0:T(8,128)(2,1)}, bf16[576,1024]{1,0:T(8,128)(2,1)S(1)}, u32[]{:S(2)}) copy-start(bf16[576,1024]{1,0:T(8,128)(2,1)S(1)} %multiply_convert_fusion.2) | copy-start | bytes 3538948
  269.9 29.5 %all-to-all-start.1 = ((bf16[8,72,1792]{2,1,0:T(8,128)(2,1)}), bf16[8,72,1792]{2,1,0:T(8,128)(2,1)S(1)}, u32[]{:S(2)}, u32[]{:S(2)}) async-start(bf16[8,72,1792]{2,1,0:T(8,128)(2,1)} %bitcast.61), calls=%async_computation.1 | async-start | bytes 4128768 | tf_op jit(solution)/shard_map/all_to_all | solution.py:31
  299.4 1.3 copy-start.3
  300.7 37.5 %all-to-all-start.2 = ((bf16[8,72,2304]{2,1,0:T(8,128)(2,1)}), bf16[8,72,2304]{2,1,0:T(8,128)(2,1)}, u32[]{:S(2)}, u32[]{:S(2)}) async-start(bf16[8,72,2304]{2,1,0:T(8,128)(2,1)} %bitcast.18), calls=%async_computation.2 | async-start | bytes 5308416 | tf_op jit(solution)/shard_map/all_to_all | solution.py:31
  311.3 5.9 %collective-permute-start.2 = (bf16[48,1792]{1,0:T(8,128)(2,1)}, bf16[48,1792]{1,0:T(8,128)(2,1)S(1)}, u32[]{:S(2)}, u32[]{:S(2)}) collective-permute-start(bf16[48,1792]{1,0:T(8,128)(2,1)} %get-tuple-element.491), channel_id=1, source_target_pairs={{0,112},{16,0},{32,16},{48,32},{64,48},{80,64},{96,80},{112,96},{1... | collective-permute-start | bytes 516104 | tf_op jit(solution)/shard_map/while/body/eval_jaxpr/ppermute | solution.py:41
  313.0 6.7 %collective-permute-start.3 = (bf16[48,1792]{1,0:T(8,128)(2,1)S(1)}, bf16[48,1792]{1,0:T(8,128)(2,1)S(1)}, u32[]{:S(2)}, u32[]{:S(2)}) collective-permute-start(bf16[48,1792]{1,0:T(8,128)(2,1)S(1)} %convert_element_type.291), channel_id=1, source_target_pairs={{0,16},{16,32},{32,48},{48,64},{64,80},{80,96},{96,112},{112,0},{1... | collective-permute-start | bytes 516104 | tf_op jit(solution)/shard_map/while/body/eval_jaxpr/ppermute | solution.py:41
  319.8 5.7 %collective-permute-start.2 = (bf16[48,1792]{1,0:T(8,128)(2,1)}, bf16[48,1792]{1,0:T(8,128)(2,1)S(1)}, u32[]{:S(2)}, u32[]{:S(2)}) collective-permute-start(bf16[48,1792]{1,0:T(8,128)(2,1)} %get-tuple-element.491), channel_id=1, source_target_pairs={{0,112},{16,0},{32,16},{48,32},{64,48},{80,64},{96,80},{112,96},{1... | collective-permute-start | bytes 516104 | tf_op jit(solution)/shard_map/while/body/eval_jaxpr/ppermute | solution.py:41
  321.0 6.7 %collective-permute-start.3 = (bf16[48,1792]{1,0:T(8,128)(2,1)S(1)}, bf16[48,1792]{1,0:T(8,128)(2,1)S(1)}, u32[]{:S(2)}, u32[]{:S(2)}) collective-permute-start(bf16[48,1792]{1,0:T(8,128)(2,1)S(1)} %convert_element_type.291), channel_id=1, source_target_pairs={{0,16},{16,32},{32,48},{48,64},{64,80},{80,96},{96,112},{112,0},{1... | collective-permute-start | bytes 516104 | tf_op jit(solution)/shard_map/while/body/eval_jaxpr/ppermute | solution.py:41
  327.8 5.7 %collective-permute-start.2 = (bf16[48,1792]{1,0:T(8,128)(2,1)}, bf16[48,1792]{1,0:T(8,128)(2,1)S(1)}, u32[]{:S(2)}, u32[]{:S(2)}) collective-permute-start(bf16[48,1792]{1,0:T(8,128)(2,1)} %get-tuple-element.491), channel_id=1, source_target_pairs={{0,112},{16,0},{32,16},{48,32},{64,48},{80,64},{96,80},{112,96},{1... | collective-permute-start | bytes 516104 | tf_op jit(solution)/shard_map/while/body/eval_jaxpr/ppermute | solution.py:41
  328.7 6.7 %collective-permute-start.3 = (bf16[48,1792]{1,0:T(8,128)(2,1)S(1)}, bf16[48,1792]{1,0:T(8,128)(2,1)S(1)}, u32[]{:S(2)}, u32[]{:S(2)}) collective-permute-start(bf16[48,1792]{1,0:T(8,128)(2,1)S(1)} %convert_element_type.291), channel_id=1, source_target_pairs={{0,16},{16,32},{32,48},{48,64},{64,80},{80,96},{96,112},{112,0},{1... | collective-permute-start | bytes 516104 | tf_op jit(solution)/shard_map/while/body/eval_jaxpr/ppermute | solution.py:41
  335.4 31.1 %collective-permute-start.18 = (bf16[48,1792]{1,0:T(8,128)(2,1)}, bf16[48,1792]{1,0:T(8,128)(2,1)}, u32[]{:S(2)}, u32[]{:S(2)}) collective-permute-start(bf16[48,1792]{1,0:T(8,128)(2,1)} %get-tuple-element.311), channel_id=1, source_target_pairs={{0,112},{16,0},{32,16},{48,32},{64,48},{80,64},{96,80},{112,96},{1... | collective-permute-start | bytes 516104 | tf_op jit(solution)/shard_map/ppermute | solution.py:41
  341.7 6.3 %collective-permute-start.4 = (bf16[48,2304]{1,0:T(8,128)(2,1)S(1)}, bf16[48,2304]{1,0:T(8,128)(2,1)S(1)}, u32[]{:S(2)}, u32[]{:S(2)}) collective-permute-start(bf16[48,2304]{1,0:T(8,128)(2,1)S(1)} %get-tuple-element.464), channel_id=1, source_target_pairs={{0,112},{16,0},{32,16},{48,32},{64,48},{80,64},{96,80},{112,96},{1... | collective-permute-start | bytes 663560 | tf_op jit(solution)/shard_map/while/body/eval_jaxpr/ppermute | solution.py:41
  343.4 7.2 %collective-permute-start.5 = (bf16[48,2304]{1,0:T(8,128)(2,1)S(1)}, bf16[48,2304]{1,0:T(8,128)(2,1)S(1)}, u32[]{:S(2)}, u32[]{:S(2)}) collective-permute-start(bf16[48,2304]{1,0:T(8,128)(2,1)S(1)} %convert_element_type.294), channel_id=1, source_target_pairs={{0,16},{16,32},{32,48},{48,64},{64,80},{80,96},{96,112},{112,0},{1... | collective-permute-start | bytes 663560 | tf_op jit(solution)/shard_map/while/body/eval_jaxpr/ppermute | solution.py:41
  350.7 6.0 %collective-permute-start.4 = (bf16[48,2304]{1,0:T(8,128)(2,1)S(1)}, bf16[48,2304]{1,0:T(8,128)(2,1)S(1)}, u32[]{:S(2)}, u32[]{:S(2)}) collective-permute-start(bf16[48,2304]{1,0:T(8,128)(2,1)S(1)} %get-tuple-element.464), channel_id=1, source_target_pairs={{0,112},{16,0},{32,16},{48,32},{64,48},{80,64},{96,80},{112,96},{1... | collective-permute-start | bytes 663560 | tf_op jit(solution)/shard_map/while/body/eval_jaxpr/ppermute | solution.py:41
  351.0 7.2 %collective-permute-start.5 = (bf16[48,2304]{1,0:T(8,128)(2,1)S(1)}, bf16[48,2304]{1,0:T(8,128)(2,1)S(1)}, u32[]{:S(2)}, u32[]{:S(2)}) collective-permute-start(bf16[48,2304]{1,0:T(8,128)(2,1)S(1)} %convert_element_type.294), channel_id=1, source_target_pairs={{0,16},{16,32},{32,48},{48,64},{64,80},{80,96},{96,112},{112,0},{1... | collective-permute-start | bytes 663560 | tf_op jit(solution)/shard_map/while/body/eval_jaxpr/ppermute | solution.py:41
  358.3 6.5 %collective-permute-start.4 = (bf16[48,2304]{1,0:T(8,128)(2,1)S(1)}, bf16[48,2304]{1,0:T(8,128)(2,1)S(1)}, u32[]{:S(2)}, u32[]{:S(2)}) collective-permute-start(bf16[48,2304]{1,0:T(8,128)(2,1)S(1)} %get-tuple-element.464), channel_id=1, source_target_pairs={{0,112},{16,0},{32,16},{48,32},{64,48},{80,64},{96,80},{112,96},{1... | collective-permute-start | bytes 663560 | tf_op jit(solution)/shard_map/while/body/eval_jaxpr/ppermute | solution.py:41
  358.5 7.2 %collective-permute-start.5 = (bf16[48,2304]{1,0:T(8,128)(2,1)S(1)}, bf16[48,2304]{1,0:T(8,128)(2,1)S(1)}, u32[]{:S(2)}, u32[]{:S(2)}) collective-permute-start(bf16[48,2304]{1,0:T(8,128)(2,1)S(1)} %convert_element_type.294), channel_id=1, source_target_pairs={{0,16},{16,32},{32,48},{48,64},{64,80},{80,96},{96,112},{112,0},{1... | collective-permute-start | bytes 663560 | tf_op jit(solution)/shard_map/while/body/eval_jaxpr/ppermute | solution.py:41
  365.7 6.0 %collective-permute-start.21 = (bf16[48,2304]{1,0:T(8,128)(2,1)S(1)}, bf16[48,2304]{1,0:T(8,128)(2,1)S(1)}, u32[]{:S(2)}, u32[]{:S(2)}) collective-permute-start(bf16[48,2304]{1,0:T(8,128)(2,1)S(1)} %get-tuple-element.313), channel_id=1, source_target_pairs={{0,112},{16,0},{32,16},{48,32},{64,48},{80,64},{96,80},{112,96},{1... | collective-permute-start | bytes 663560 | tf_op jit(solution)/shard_map/ppermute | solution.py:41
where the time goes:
time: 380 us; the launch traced here: 373 us
  waiting for transfers between devices  246 us (65%)
  starting transfers between devices  56.6 us (15%)
  matrix products  43.7 us (12%)
  local copies, waits for them, and re-layouts  15.9 us (4%)
  other arithmetic  10.3 us (3%)
    ppermute x13, waiting for transfers between devices, swap(): return lax.ppermute(block, axis, [(0, 1), (1, 0)])  157 us
    ppermute x21, waiting for transfers between devices, along_z(): return lax.ppermute(block, 'z', [(i, (i + step) % NZ) for i in range(NZ)])  70.7 us
    ppermute x21, starting transfers between devices, along_z(): return lax.ppermute(block, 'z', [(i, (i + step) % NZ) for i in range(NZ)])  28.5 us
    all_to_all x3, waiting for transfers between devices, exchange(): lax.all_to_all(block, AXES, 0, 0, axis_index_groups=plane_groups(), tiled...  18.3 us
    all_to_all x3, starting transfers between devices, exchange(): lax.all_to_all(block, AXES, 0, 0, axis_index_groups=plane_groups(), tiled...  18.2 us
    dot_general x2, matrix products, local(): lax.dot_general(hidden, downs[c], (((1,), (1,)), ((), ())), preferred_ele...  11.6 us
    ppermute x13, starting transfers between devices, swap(): return lax.ppermute(block, axis, [(0, 1), (1, 0)])  9.88 us
    dot_general x1, matrix products, local(): gate_part = jnp.dot(arrived, gate, preferred_element_type=jnp.float32)  9.18 us
  transfers between devices with their start and end apart: 37, of which 23 were waited for; matrix products, arithmetic and copies ran while one was open for 13% of the time, Pallas kernels for 0%

commit v1 on v0

--- a/solution.py
+++ b/solution.py
@@ -8,8 +8,8 @@
 AXES = ("yl", "z", "x", "yh", "core")
 CAP = 9
 EXTRA = 128
-OUT = (1792, 2304)
-UP = 1024
+OUT = (2304, 1792)
+UP = 2048
 LOOPED = (True, True)
 
 
@@ -79,18 +79,18 @@
     cap = CAP * NZ
 
     own_gate, own_up, own_down = gate_weight[0], up_weight[0], down_weight[0]
-    near_gate, near_up, near_down = swap(own_gate, "core"), swap(own_up, "core"), swap(own_down, "core")
 
-    def pieces(own, near, start, size):
+    def pieces(own, start, size):
         own = own[start : start + size]
         far = swap(own, "yh")
+        near = swap(own, "core")
         hop = swap(far, "core")
-        return jnp.concatenate([own, near[start : start + size], far, hop], axis=1)
+        return jnp.concatenate([own, near, far, hop], axis=1)
 
-    gate = pieces(own_gate, near_gate, 0, width)
-    up0 = pieces(own_up, near_up, 0, UP)
-    up1 = pieces(own_up, near_up, UP, width - UP)
-    downs = [pieces(own_down, near_down, 0, OUT[0]), pieces(own_down, near_down, OUT[0], OUT[1])]
+    gate = pieces(own_gate, 0, width)
+    up0 = pieces(own_up, 0, UP)
+    up1 = pieces(own_up, UP, width - UP)
+    downs = [pieces(own_down, 0, OUT[0]), pieces(own_down, OUT[0], OUT[1])]
 
     notes = jnp.concatenate([expert_ids.astype(jnp.bfloat16)] + parts_of(gate_values, 2), axis=1)
     notes = jnp.pad(notes, ((0, 0), (0, EXTRA - notes.shape[1])))

time: 380 us -> 369 us (0.971)
  the two profiles are of different devices: /device:TPU:14 before, /device:TPU:2 now
where the time goes in v1:
time: 369 us; the launch traced here: 368 us
  waiting for transfers between devices  239 us (65%)
  starting transfers between devices  61.9 us (17%)
  matrix products  42.4 us (11%)
  local copies, waits for them, and re-layouts  14.1 us (4%)
  other arithmetic  10.3 us (3%)
    ppermute x15, waiting for transfers between devices, swap(): return lax.ppermute(block, axis, [(0, 1), (1, 0)])  140 us
    ppermute x21, waiting for transfers between devices, along_z(): return lax.ppermute(block, 'z', [(i, (i + step) % NZ) for i in range(NZ)])  78.5 us
    ppermute x21, starting transfers between devices, along_z(): return lax.ppermute(block, 'z', [(i, (i + step) % NZ) for i in range(NZ)])  28.2 us
    all_to_all x3, starting transfers between devices, exchange(): lax.all_to_all(block, AXES, 0, 0, axis_index_groups=plane_groups(), tiled...  21.7 us
    all_to_all x3, waiting for transfers between devices, exchange(): lax.all_to_all(block, AXES, 0, 0, axis_index_groups=plane_groups(), tiled...  20.6 us
    ppermute x15, starting transfers between devices, swap(): return lax.ppermute(block, axis, [(0, 1), (1, 0)])  12 us
    dot_general x2, matrix products, local(): lax.dot_general(hidden, downs[c], (((1,), (1,)), ((), ())), preferred_ele...  10.3 us
    dot_general x1, matrix products, local(): gate_part = jnp.dot(arrived, gate, preferred_element_type=jnp.float32)  9.3 us
  transfers between devices with their start and end apart: 39, of which 23 were waited for; matrix products, arithmetic and copies ran while one was open for 12% of the time, Pallas kernels for 0%

profile of v1, /device:TPU:2, one launch (start us, length us, event | category | flops | bytes accessed | tf_op | source)
XLA Modules:
  0.0 368.0 jit_solution(1183453933836703812)
XLA Ops:
  1.6 1.0 fusion.59
  2.6 1.9 broadcast_in_dim.41
  4.5 42.9 %while.51 = (s32[]{:T(128)}, bf16[384,4224]{1,0:T(8,128)(2,1)}, bf16[48,4224]{1,0:T(8,128)(2,1)S(1)}, bf16[48,4224]{1,0:T(8,128)(2,1)S(1)}, s32[]{:T(128)}, /*in...) while((s32[]{:T(128)}, bf16[384,4224]{1,0:T(8,128)(2,1)}, bf16[48,4224]{1,0:T(8,128)(2,1)S(1)}, ...), condition=%wide.region_1.2_spmd, body=%wide.region_0.1_spmd.sunk | while | flops 12 | bytes 6488369 | solution.py:108
  4.5 1.9 collective-permute-start
  6.4 3.9 %collective-permute-start.1 = (bf16[48,4224]{1,0:T(8,128)(2,1)S(1)}, bf16[48,4224]{1,0:T(8,128)(2,1)S(1)}, u32[]{:S(2)}, u32[]{:S(2)}) collective-permute-start(bf16[48,4224]{1,0:T(8,128)(2,1)S(1)} %get-tuple-element.439), channel_id=1, source_target_pairs={{0,112},{16,0},{32,16},{48,32},{64,48},{80,64},{96,80},{112,96},{1... | collective-permute-start | bytes 1216520 | tf_op jit(solution)/shard_map/while/body/eval_jaxpr/ppermute | solution.py:41
  10.4 9.4 %collective-permute-done = bf16[48,4224]{1,0:T(8,128)(2,1)S(1)} collective-permute-done((bf16[48,4224]{1,0:T(8,128)(2,1)S(1)}, bf16[48,4224]{1,0:T(8,128)(2,1)S(1)}, u32[]{:S(2)}, u32[]{:S(2)}) %collective-permute-start) | collective-permute-done | bytes 405536 | tf_op jit(solution)/shard_map/while/body/eval_jaxpr/ppermute | solution.py:41
  21.4 3.2 collective-permute-start.1
  24.6 8.5 %collective-permute-done = bf16[48,4224]{1,0:T(8,128)(2,1)S(1)} collective-permute-done((bf16[48,4224]{1,0:T(8,128)(2,1)S(1)}, bf16[48,4224]{1,0:T(8,128)(2,1)S(1)}, u32[]{:S(2)}, u32[]{:S(2)}) %collective-permute-start) | collective-permute-done | bytes 405536 | tf_op jit(solution)/shard_map/while/body/eval_jaxpr/ppermute | solution.py:41
  34.8 1.8 collective-permute-start
  36.7 1.4 collective-permute-start.1
  38.1 7.7 %collective-permute-done = bf16[48,4224]{1,0:T(8,128)(2,1)S(1)} collective-permute-done((bf16[48,4224]{1,0:T(8,128)(2,1)S(1)}, bf16[48,4224]{1,0:T(8,128)(2,1)S(1)}, u32[]{:S(2)}, u32[]{:S(2)}) %collective-permute-start) | collective-permute-done | bytes 405536 | tf_op jit(solution)/shard_map/while/body/eval_jaxpr/ppermute | solution.py:41
  47.4 1.5 collective-permute-start.6
  48.9 8.5 %collective-permute-done.6 = bf16[48,4224]{1,0:T(8,128)(2,1)S(1)} collective-permute-done((bf16[48,4224]{1,0:T(8,128)(2,1)S(1)}, bf16[48,4224]{1,0:T(8,128)(2,1)S(1)}, u32[]{:S(2)}, u32[]{:S(2)}) %collective-permute-start.6) | collective-permute-done | bytes 405536 | tf_op jit(solution)/shard_map/ppermute | solution.py:41
  60.9 6.3 %convolution_convert_fusion = bf16[576,4224]{1,0:T(8,128)(2,1)} fusion(pred[384,576]{0,1:T(32,128)(4,1)S(1)} %bitcast_compare_fusion, bf16[384,4224]{1,0:T(8,128)(2,1)} %pad_dynamic-update-slice_fusion), kind=kOutput, calls=%fused_computation.14 | convolution fusion | flops 1870995456 | bytes 8331264 | tf_op jit(solution)/shard_map/dot_general | solution.py:135
  67.2 5.8 %all-to-all-start = ((bf16[8,72,4224]{2,1,0:T(8,128)(2,1)}), bf16[8,72,4224]{2,1,0:T(8,128)(2,1)}, u32[]{:S(2)}, u32[]{:S(2)}) async-start(bf16[8,72,4224]{2,1,0:T(8,128)(2,1)} %bitcast.53), calls=%async_computation | async-start | bytes 9732096 | tf_op jit(solution)/shard_map/all_to_all | solution.py:31
  73.0 2.9 collective-permute-start.8
  75.9 70.6 %collective-permute-done.8 = bf16[4096,256]{1,0:T(8,128)(2,1)} collective-permute-done((bf16[4096,256]{1,0:T(8,128)(2,1)}, bf16[4096,256]{1,0:T(8,128)(2,1)}, u32[]{:S(2)}, u32[]{:S(2)}) %collective-permute-start.8) | collective-permute-done | bytes 2097184 | tf_op jit(solution)/shard_map/ppermute | solution.py:37
  146.5 3.0 slice_bitcast_fusion.2
  149.6 1.2 collective-permute-start.14
  151.0 1.0 slice_bitcast_fusion.3
  152.1 2.4 collective-permute-start.11
  154.5 22.9 %collective-permute-done.14 = bf16[2048,256]{1,0:T(8,128)(2,1)} collective-permute-done((bf16[2048,256]{1,0:T(8,128)(2,1)}, bf16[2048,256]{1,0:T(8,128)(2,1)}, u32[]{:S(2)}, u32[]{:S(2)}) %collective-permute-start.14) | collective-permute-done | bytes 1048608 | tf_op jit(solution)/shard_map/ppermute | solution.py:37
  177.4 1.2 collective-permute-start.17
  178.7 9.3 %fusion = f32[576,1024]{1,0:T(8,128)S(1)} fusion(bf16[4096,256]{1,0:T(8,128)(2,1)} %collective-permute-done.9, bf16[4096,256]{1,0:T(8,128)(2,1)} %collective-permute-done.8, bf16[4096,256]{1,0:T(8,128)(2,1)} %collective-permute-done.7, bf16[4096,256]{1,0:T(8,128)(2,1)} %bitcast.60, bf16[576,4224]{1,0:T(8,128)(2,1)} %bitcast.7), kind=kOutput, calls=%fused_computation.6 | convolution fusion | flops 4865392640 | bytes 15466496 | tf_op jit(solution)/shard_map/dot_general | solution.py:144
  188.0 1.1 select_reduce_fusion
  189.7 2.3 collective-permute-start.21
  192.0 7.8 %collective-permute-done.11 = bf16[2048,256]{1,0:T(8,128)(2,1)S(1)} collective-permute-done((bf16[2048,256]{1,0:T(8,128)(2,1)}, bf16[2048,256]{1,0:T(8,128)(2,1)S(1)}, u32[]{:S(2)}, u32[]{:S(2)}) %collective-permute-start.11) | collective-permute-done | bytes 1048608 | tf_op jit(solution)/shard_map/ppermute | solution.py:37
  199.8 5.4 %fusion.25 = f32[576,1024]{1,0:T(8,128)S(1)} fusion(bf16[2048,256]{1,0:T(8,128)(2,1)} %collective-permute-done.15, bf16[2048,256]{1,0:T(8,128)(2,1)} %collective-permute-done.14, bf16[2048,256]{1,0:T(8,128)(2,1)} %collective-permute-done.13, bf16[2048,256]{1,0:T(8,128)(2,1)} %get-tuple-element.344, bf16[576,4224]{1,0:T(8,128)(2,1)} %bitcast.7), kind=kOutput, calls=%fused_computation.34 | convolution fusion | flops 2432696320 | bytes 8912896 | tf_op jit(solution)/shard_map/dot_general | solution.py:145
  205.8 38.5 %collective-permute-done.21 = bf16[1792,256]{1,0:T(8,128)(2,1)S(1)} collective-permute-done((bf16[1792,256]{1,0:T(8,128)(2,1)S(1)}, bf16[1792,256]{1,0:T(8,128)(2,1)S(1)}, u32[]{:S(2)}, u32[]{:S(2)}) %collective-permute-start.21) | collective-permute-done | bytes 917536 | tf_op jit(solution)/shard_map/ppermute | solution.py:37
  244.9 4.6 %multiply_convert_fusion.2 = bf16[576,1024]{1,0:T(8,128)(2,1)S(1)} fusion(f32[576,1024]{1,0:T(8,128)S(1)} %fusion.25, f32[576,1024]{1,0:T(8,128)S(1)} %fusion, bf16[2048,256]{1,0:T(8,128)(2,1)S(1)} %collective-permute-done.12, bf16[2048,256]{1,0:T(8,128)(2,1)S(1)} %collective-permute-done.11, bf16[2048,256]{1,0:T(8,128)(2,1)S(1)} %collective-permute-done.10, ...), kind=kOutput, calls=%fused_computation.55 | convolution fusion | flops 2436825088 | bytes 12451840 | tf_op jit(solution)/shard_map/dot_general | solution.py:146
  249.5 3.9 %multiply_convert_fusion.1 = bf16[576,1792]{1,0:T(8,128)(2,1)} fusion(bf16[576,1024]{1,0:T(8,128)(2,1)S(1)} %multiply_convert_fusion.2, bf16[1792,256]{1,0:T(8,128)(2,1)S(1)} %collective-permute-done.22, bf16[1792,256]{1,0:T(8,128)(2,1)S(1)} %collective-permute-done.21, bf16[1792,256]{1,0:T(8,128)(2,1)S(1)} %collective-permute-done.20, ...), kind=kOutput, calls=%fused_computation.42 | convolution fusion | flops 2130673664 | bytes 6916352 | tf_op jit(solution)/shard_map/dot_general | solution.py:151
  253.4 10.4 %all-to-all-start.2 = ((bf16[8,72,1792]{2,1,0:T(8,128)(2,1)}), bf16[8,72,1792]{2,1,0:T(8,128)(2,1)S(1)}, u32[]{:S(2)}, u32[]{:S(2)}) async-start(bf16[8,72,1792]{2,1,0:T(8,128)(2,1)} %bitcast.57), calls=%async_computation.2 | async-start | bytes 4128768 | tf_op jit(solution)/shard_map/all_to_all | solution.py:31
  263.8 6.4 %multiply_convert_fusion = bf16[576,2304]{1,0:T(8,128)(2,1)} fusion(bf16[576,1024]{1,0:T(8,128)(2,1)} %copy-done.4, bf16[2304,256]{1,0:T(8,128)(2,1)} %collective-permute-done.18, bf16[2304,256]{1,0:T(8,128)(2,1)} %collective-permute-done.17, bf16[2304,256]{1,0:T(8,128)(2,1)} %collective-permute-done.16, bf16[2304,256]{1,0:T(8,128)(2,1)S(1)} %slice_bitcast_fusion, ...), kind=kOutput, calls=%fused_computation.15 | convolution fusion | flops 2739437568 | bytes 8554752 | tf_op jit(solution)/shard_map/dot_general | solution.py:151
  270.2 19.5 %all-to-all-done.2 = bf16[8,72,1792]{2,1,0:T(8,128)(2,1)S(1)} async-done(((bf16[8,72,1792]{2,1,0:T(8,128)(2,1)}), bf16[8,72,1792]{2,1,0:T(8,128)(2,1)S(1)}, u32[]{:S(2)}, u32[]{:S(2)}) %all-to-all-start.2) | async-done | bytes 2064416 | tf_op jit(solution)/shard_map/all_to_all | solution.py:31
  289.8 1.3 copy-done.1
  291.1 5.4 %all-to-all-start.1 = ((bf16[8,72,2304]{2,1,0:T(8,128)(2,1)}), bf16[8,72,2304]{2,1,0:T(8,128)(2,1)}, u32[]{:S(2)}, u32[]{:S(2)}) async-start(bf16[8,72,2304]{2,1,0:T(8,128)(2,1)} %bitcast.12), calls=%async_computation.1 | async-start | bytes 5308416 | tf_op jit(solution)/shard_map/all_to_all | solution.py:31
  296.5 2.9 fusion.41
  300.1 26.4 %while.53 = (s32[]{:T(128)}, bf16[48,1792]{1,0:T(8,128)(2,1)}, f32[48,1792]{1,0:T(8,128)S(1)}, bf16[8,48,1792]{2,1,0:T(8,128)(2,1)S(1)}, s32[]{:T(128)}, /*index=5*/s32[]{:T(128)}, s32[]{:T(128)}, s32[]{:T(128)}, s32[]{:T(128)}) while((s32[]{:T(128)}, bf16[48,1792]{1,0:T(8,128)(2,1)}, f32[48,1792]{1,0:T(8,128)S(1)}, ...), condition=%wide.region_8.9_spmd, body=%wide.region_7.8_spmd.sunk | while | flops 688137 | bytes 3096845 | solution.py:66
  300.1 1.6 collective-permute-start.4
  302.3 5.3 %collective-permute-done.4 = bf16[48,1792]{1,0:T(8,128)(2,1)S(1)} collective-permute-done((bf16[48,1792]{1,0:T(8,128)(2,1)}, bf16[48,1792]{1,0:T(8,128)(2,1)S(1)}, u32[]{:S(2)}, u32[]{:S(2)}) %collective-permute-start.4) | collective-permute-done | bytes 172064 | tf_op jit(solution)/shard_map/while/body/eval_jaxpr/ppermute | solution.py:41
  308.3 1.7 collective-permute-done.5
  310.0 1.2 collective-permute-start.4
  311.2 1.0 collective-permute-start.5
  312.2 4.1 %collective-permute-done.4 = bf16[48,1792]{1,0:T(8,128)(2,1)S(1)} collective-permute-done((bf16[48,1792]{1,0:T(8,128)(2,1)}, bf16[48,1792]{1,0:T(8,128)(2,1)S(1)}, u32[]{:S(2)}, u32[]{:S(2)}) %collective-permute-start.4) | collective-permute-done | bytes 172064 | tf_op jit(solution)/shard_map/while/body/eval_jaxpr/ppermute | solution.py:41
  317.1 1.5 collective-permute-done.5
  318.6 1.2 collective-permute-start.4
  319.8 1.0 collective-permute-start.5
  320.8 3.5 collective-permute-done.4
  325.0 1.5 collective-permute-done.5
  326.6 1.0 collective-permute-start.23
  327.5 1.0 all-to-all-done.1
  328.6 3.4 fusion.16
  332.0 28.8 %while.52 = (s32[]{:T(128)}, bf16[48,2304]{1,0:T(8,128)(2,1)S(1)}, f32[48,2304]{1,0:T(8,128)S(1)}, bf16[8,48,2304]{2,1,0:T(8,128)(2,1)S(1)}, s32[]{:T(128)}, /*index=5*/s32[]{:T(128)}, s32[]{:T(128)}, s32[]{:T(128)}, s32[]{:T(128)}) while((s32[]{:T(128)}, bf16[48,2304]{1,0:T(8,128)(2,1)S(1)}, f32[48,2304]{1,0:T(8,128)S(1)}, ...), condition=%wide.region_6.7_spmd, body=%wide.region_5.6_spmd.sunk | while | flops 884745 | bytes 3981581 | solution.py:66
  332.0 1.7 collective-permute-start.2
  334.2 5.1 %collective-permute-done.2 = bf16[48,2304]{1,0:T(8,128)(2,1)S(1)} collective-permute-done((bf16[48,2304]{1,0:T(8,128)(2,1)S(1)}, bf16[48,2304]{1,0:T(8,128)(2,1)S(1)}, u32[]{:S(2)}, u32[]{:S(2)}) %collective-permute-start.2) | collective-permute-done | bytes 221216 | tf_op jit(solution)/shard_map/while/body/eval_jaxpr/ppermute | solution.py:41
  339.3 3.2 collective-permute-done.3
  342.7 2.1 collective-permute-start.3
  344.8 5.8 %collective-permute-done.2 = bf16[48,2304]{1,0:T(8,128)(2,1)S(1)} collective-permute-done((bf16[48,2304]{1,0:T(8,128)(2,1)S(1)}, bf16[48,2304]{1,0:T(8,128)(2,1)S(1)}, u32[]{:S(2)}, u32[]{:S(2)}) %collective-permute-start.2) | collective-permute-done | bytes 221216 | tf_op jit(solution)/shard_map/while/body/eval_jaxpr/ppermute | solution.py:41
  350.7 1.3 collective-permute-done.3
  352.4 1.9 collective-permute-start.3
  354.3 5.0 %collective-permute-done.2 = bf16[48,2304]{1,0:T(8,128)(2,1)S(1)} collective-permute-done((bf16[48,2304]{1,0:T(8,128)(2,1)S(1)}, bf16[48,2304]{1,0:T(8,128)(2,1)S(1)}, u32[]{:S(2)}, u32[]{:S(2)}) %collective-permute-start.2) | collective-permute-done | bytes 221216 | tf_op jit(solution)/shard_map/while/body/eval_jaxpr/ppermute | solution.py:41
  359.3 1.5 collective-permute-done.3
  361.2 0.9 add_convert_fusion.1
  362.2 5.0 %collective-permute-done.19 = bf16[48,2304]{1,0:T(8,128)(2,1)S(1)} collective-permute-done((bf16[48,2304]{1,0:T(8,128)(2,1)S(1)}, bf16[48,2304]{1,0:T(8,128)(2,1)S(1)}, u32[]{:S(2)}, u32[]{:S(2)}) %collective-permute-start.19) | collective-permute-done | bytes 221216 | tf_op jit(solution)/shard_map/ppermute | solution.py:41
  (98 shorter events, 18.0 us)
Async XLA Ops:
  4.5 15.2 %collective-permute-start = (bf16[48,4224]{1,0:T(8,128)(2,1)S(1)}, bf16[48,4224]{1,0:T(8,128)(2,1)S(1)}, u32[]{:S(2)}, u32[]{:S(2)}) collective-permute-start(bf16[48,4224]{1,0:T(8,128)(2,1)S(1)} %get-tuple-element.438), channel_id=1, source_target_pairs={{0,16},{16,32},{32,48},{48,64},{64,80},{80,96},{96,112},{112,0},{1... | collective-permute-start | bytes 1216520 | tf_op jit(solution)/shard_map/while/body/eval_jaxpr/ppermute | solution.py:41
  6.4 13.3 %collective-permute-start.1 = (bf16[48,4224]{1,0:T(8,128)(2,1)S(1)}, bf16[48,4224]{1,0:T(8,128)(2,1)S(1)}, u32[]{:S(2)}, u32[]{:S(2)}) collective-permute-start(bf16[48,4224]{1,0:T(8,128)(2,1)S(1)} %get-tuple-element.439), channel_id=1, source_target_pairs={{0,112},{16,0},{32,16},{48,32},{64,48},{80,64},{96,80},{112,96},{1... | collective-permute-start | bytes 1216520 | tf_op jit(solution)/shard_map/while/body/eval_jaxpr/ppermute | solution.py:41
  21.4 11.8 %collective-permute-start = (bf16[48,4224]{1,0:T(8,128)(2,1)S(1)}, bf16[48,4224]{1,0:T(8,128)(2,1)S(1)}, u32[]{:S(2)}, u32[]{:S(2)}) collective-permute-start(bf16[48,4224]{1,0:T(8,128)(2,1)S(1)} %get-tuple-element.438), channel_id=1, source_target_pairs={{0,16},{16,32},{32,48},{48,64},{64,80},{80,96},{96,112},{112,0},{1... | collective-permute-start | bytes 1216520 | tf_op jit(solution)/shard_map/while/body/eval_jaxpr/ppermute | solution.py:41
  21.4 11.8 %collective-permute-start.1 = (bf16[48,4224]{1,0:T(8,128)(2,1)S(1)}, bf16[48,4224]{1,0:T(8,128)(2,1)S(1)}, u32[]{:S(2)}, u32[]{:S(2)}) collective-permute-start(bf16[48,4224]{1,0:T(8,128)(2,1)S(1)} %get-tuple-element.439), channel_id=1, source_target_pairs={{0,112},{16,0},{32,16},{48,32},{64,48},{80,64},{96,80},{112,96},{1... | collective-permute-start | bytes 1216520 | tf_op jit(solution)/shard_map/while/body/eval_jaxpr/ppermute | solution.py:41
  34.8 10.9 %collective-permute-start = (bf16[48,4224]{1,0:T(8,128)(2,1)S(1)}, bf16[48,4224]{1,0:T(8,128)(2,1)S(1)}, u32[]{:S(2)}, u32[]{:S(2)}) collective-permute-start(bf16[48,4224]{1,0:T(8,128)(2,1)S(1)} %get-tuple-element.438), channel_id=1, source_target_pairs={{0,16},{16,32},{32,48},{48,64},{64,80},{80,96},{96,112},{112,0},{1... | collective-permute-start | bytes 1216520 | tf_op jit(solution)/shard_map/while/body/eval_jaxpr/ppermute | solution.py:41
  36.7 9.1 %collective-permute-start.1 = (bf16[48,4224]{1,0:T(8,128)(2,1)S(1)}, bf16[48,4224]{1,0:T(8,128)(2,1)S(1)}, u32[]{:S(2)}, u32[]{:S(2)}) collective-permute-start(bf16[48,4224]{1,0:T(8,128)(2,1)S(1)} %get-tuple-element.439), channel_id=1, source_target_pairs={{0,112},{16,0},{32,16},{48,32},{64,48},{80,64},{96,80},{112,96},{1... | collective-permute-start | bytes 1216520 | tf_op jit(solution)/shard_map/while/body/eval_jaxpr/ppermute | solution.py:41
  47.4 10.0 %collective-permute-start.6 = (bf16[48,4224]{1,0:T(8,128)(2,1)S(1)}, bf16[48,4224]{1,0:T(8,128)(2,1)S(1)}, u32[]{:S(2)}, u32[]{:S(2)}) collective-permute-start(bf16[48,4224]{1,0:T(8,128)(2,1)S(1)} %get-tuple-element.310), channel_id=1, source_target_pairs={{0,16},{16,32},{32,48},{48,64},{64,80},{80,96},{96,112},{112,0},{1... | collective-permute-start | bytes 1216520 | tf_op jit(solution)/shard_map/ppermute | solution.py:41
  67.2 111.5 %all-to-all-start = ((bf16[8,72,4224]{2,1,0:T(8,128)(2,1)}), bf16[8,72,4224]{2,1,0:T(8,128)(2,1)}, u32[]{:S(2)}, u32[]{:S(2)}) async-start(bf16[8,72,4224]{2,1,0:T(8,128)(2,1)} %bitcast.53), calls=%async_computation | async-start | bytes 9732096 | tf_op jit(solution)/shard_map/all_to_all | solution.py:31
  73.0 78.0 %copy-start = (bf16[1,4096,256]{2,1,0:T(8,128)(2,1)S(1)}, bf16[1,4096,256]{2,1,0:T(8,128)(2,1)}, u32[]{:S(2)}) copy-start(bf16[1,4096,256]{2,1,0:T(8,128)(2,1)} %param.17) | copy-start | bytes 6291460
  73.0 73.5 %collective-permute-start.8 = (bf16[4096,256]{1,0:T(8,128)(2,1)}, bf16[4096,256]{1,0:T(8,128)(2,1)}, u32[]{:S(2)}, u32[]{:S(2)}) collective-permute-start(bf16[4096,256]{1,0:T(8,128)(2,1)} %bitcast.58), channel_id=1, source_target_pairs={{0,2},{2,0},{1,3},{3,1},{4,6},{6,4},{5,7},{7,5},{8,10},{10,8},{9,1... | collective-permute-start | bytes 6291464 | tf_op jit(solution)/shard_map/ppermute | solution.py:37
  75.9 102.7 %collective-permute-start.7 = (bf16[4096,256]{1,0:T(8,128)(2,1)}, bf16[4096,256]{1,0:T(8,128)(2,1)}, u32[]{:S(2)}, u32[]{:S(2)}) collective-permute-start(bf16[4096,256]{1,0:T(8,128)(2,1)} %bitcast.59), channel_id=1, source_target_pairs={{0,1},{1,0},{2,3},{3,2},{4,5},{5,4},{6,7},{7,6},{8,9},{9,8},{10,11... | collective-permute-start | bytes 6291464 | tf_op jit(solution)/shard_map/ppermute | solution.py:37
  146.5 32.1 %collective-permute-start.9 = (bf16[4096,256]{1,0:T(8,128)(2,1)}, bf16[4096,256]{1,0:T(8,128)(2,1)}, u32[]{:S(2)}, u32[]{:S(2)}) collective-permute-start(bf16[4096,256]{1,0:T(8,128)(2,1)} %collective-permute-done.8), channel_id=1, source_target_pairs={{0,1},{1,0},{2,3},{3,2},{4,5},{5,4},{6,7},{7,6},{8,9},{9,8},{10,11... | collective-permute-start | bytes 6291464 | tf_op jit(solution)/shard_map/ppermute | solution.py:37
  149.6 27.9 %collective-permute-start.14 = (bf16[2048,256]{1,0:T(8,128)(2,1)}, bf16[2048,256]{1,0:T(8,128)(2,1)}, u32[]{:S(2)}, u32[]{:S(2)}) collective-permute-start(bf16[2048,256]{1,0:T(8,128)(2,1)} %get-tuple-element.344), channel_id=1, source_target_pairs={{0,2},{2,0},{1,3},{3,1},{4,6},{6,4},{5,7},{7,5},{8,10},{10,8},{9,1... | collective-permute-start | bytes 3145736 | tf_op jit(solution)/shard_map/ppermute | solution.py:37
  150.8 38.9 %collective-permute-start.13 = (bf16[2048,256]{1,0:T(8,128)(2,1)}, bf16[2048,256]{1,0:T(8,128)(2,1)}, u32[]{:S(2)}, u32[]{:S(2)}) collective-permute-start(bf16[2048,256]{1,0:T(8,128)(2,1)} %get-tuple-element.344), channel_id=1, source_target_pairs={{0,1},{1,0},{2,3},{3,2},{4,5},{5,4},{6,7},{7,6},{8,9},{9,8},{10,11... | collective-permute-start | bytes 3145736 | tf_op jit(solution)/shard_map/ppermute | solution.py:37
  152.1 47.7 %collective-permute-start.11 = (bf16[2048,256]{1,0:T(8,128)(2,1)}, bf16[2048,256]{1,0:T(8,128)(2,1)S(1)}, u32[]{:S(2)}, u32[]{:S(2)}) collective-permute-start(bf16[2048,256]{1,0:T(8,128)(2,1)} %get-tuple-element.343), channel_id=1, source_target_pairs={{0,2},{2,0},{1,3},{3,1},{4,6},{6,4},{5,7},{7,5},{8,10},{10,8},{9,1... | collective-permute-start | bytes 3145736 | tf_op jit(solution)/shard_map/ppermute | solution.py:37
  177.4 67.4 %collective-permute-start.17 = (bf16[2304,256]{1,0:T(8,128)(2,1)S(1)}, bf16[2304,256]{1,0:T(8,128)(2,1)}, u32[]{:S(2)}, u32[]{:S(2)}) collective-permute-start(bf16[2304,256]{1,0:T(8,128)(2,1)S(1)} %slice_bitcast_fusion), channel_id=1, source_target_pairs={{0,2},{2,0},{1,3},{3,1},{4,6},{6,4},{5,7},{7,5},{8,10},{10,8},{9,1... | collective-permute-start | bytes 3538952 | tf_op jit(solution)/shard_map/ppermute | solution.py:37
  178.7 21.1 %collective-permute-start.15 = (bf16[2048,256]{1,0:T(8,128)(2,1)}, bf16[2048,256]{1,0:T(8,128)(2,1)}, u32[]{:S(2)}, u32[]{:S(2)}) collective-permute-start(bf16[2048,256]{1,0:T(8,128)(2,1)} %collective-permute-done.14), channel_id=1, source_target_pairs={{0,1},{1,0},{2,3},{3,2},{4,5},{5,4},{6,7},{7,6},{8,9},{9,8},{10,11... | collective-permute-start | bytes 3145736 | tf_op jit(solution)/shard_map/ppermute | solution.py:37
  178.7 10.4 %copy-start.2 = (bf16[2048,256]{1,0:T(8,128)(2,1)S(1)}, bf16[2048,256]{1,0:T(8,128)(2,1)}, u32[]{:S(2)}) copy-start(bf16[2048,256]{1,0:T(8,128)(2,1)} %get-tuple-element.343) | copy-start | bytes 3145732
  178.7 11.0 %copy-start.3 = (bf16[1792,256]{1,0:T(8,128)(2,1)S(1)}, bf16[1792,256]{1,0:T(8,128)(2,1)}, u32[]{:S(2)}) copy-start(bf16[1792,256]{1,0:T(8,128)(2,1)} %slice_bitcast_fusion.3) | copy-start | bytes 2752516
  189.1 55.2 %collective-permute-start.10 = (bf16[2048,256]{1,0:T(8,128)(2,1)S(1)}, bf16[2048,256]{1,0:T(8,128)(2,1)S(1)}, u32[]{:S(2)}, u32[]{:S(2)}) collective-permute-start(bf16[2048,256]{1,0:T(8,128)(2,1)S(1)} %copy-done.2), channel_id=1, source_target_pairs={{0,1},{1,0},{2,3},{3,2},{4,5},{5,4},{6,7},{7,6},{8,9},{9,8},{10,11... | collective-permute-start | bytes 3145736 | tf_op jit(solution)/shard_map/ppermute | solution.py:37
  189.7 54.6 %collective-permute-start.21 = (bf16[1792,256]{1,0:T(8,128)(2,1)S(1)}, bf16[1792,256]{1,0:T(8,128)(2,1)S(1)}, u32[]{:S(2)}, u32[]{:S(2)}) collective-permute-start(bf16[1792,256]{1,0:T(8,128)(2,1)S(1)} %copy-done.3), channel_id=1, source_target_pairs={{0,2},{2,0},{1,3},{3,1},{4,6},{6,4},{5,7},{7,5},{8,10},{10,8},{9,1... | collective-permute-start | bytes 2752520 | tf_op jit(solution)/shard_map/ppermute | solution.py:37
  199.8 45.1 %collective-permute-start.12 = (bf16[2048,256]{1,0:T(8,128)(2,1)S(1)}, bf16[2048,256]{1,0:T(8,128)(2,1)S(1)}, u32[]{:S(2)}, u32[]{:S(2)}) collective-permute-start(bf16[2048,256]{1,0:T(8,128)(2,1)S(1)} %collective-permute-done.11), channel_id=1, source_target_pairs={{0,1},{1,0},{2,3},{3,2},{4,5},{5,4},{6,7},{7,6},{8,9},{9,8},{10,11... | collective-permute-start | bytes 3145736 | tf_op jit(solution)/shard_map/ppermute | solution.py:37
  205.3 58.5 %collective-permute-start.16 = (bf16[2304,256]{1,0:T(8,128)(2,1)S(1)}, bf16[2304,256]{1,0:T(8,128)(2,1)}, u32[]{:S(2)}, u32[]{:S(2)}) collective-permute-start(bf16[2304,256]{1,0:T(8,128)(2,1)S(1)} %slice_bitcast_fusion), channel_id=1, source_target_pairs={{0,1},{1,0},{2,3},{3,2},{4,5},{5,4},{6,7},{7,6},{8,9},{9,8},{10,11... | collective-permute-start | bytes 3538952 | tf_op jit(solution)/shard_map/ppermute | solution.py:37
  244.3 5.2 %collective-permute-start.20 = (bf16[1792,256]{1,0:T(8,128)(2,1)S(1)}, bf16[1792,256]{1,0:T(8,128)(2,1)S(1)}, u32[]{:S(2)}, u32[]{:S(2)}) collective-permute-start(bf16[1792,256]{1,0:T(8,128)(2,1)S(1)} %copy-done.3), channel_id=1, source_target_pairs={{0,1},{1,0},{2,3},{3,2},{4,5},{5,4},{6,7},{7,6},{8,9},{9,8},{10,11... | collective-permute-start | bytes 2752520 | tf_op jit(solution)/shard_map/ppermute | solution.py:37
  244.3 5.2 %collective-permute-start.22 = (bf16[1792,256]{1,0:T(8,128)(2,1)S(1)}, bf16[1792,256]{1,0:T(8,128)(2,1)S(1)}, u32[]{:S(2)}, u32[]{:S(2)}) collective-permute-start(bf16[1792,256]{1,0:T(8,128)(2,1)S(1)} %collective-permute-done.21), channel_id=1, source_target_pairs={{0,1},{1,0},{2,3},{3,2},{4,5},{5,4},{6,7},{7,6},{8,9},{9,8},{10,11... | collective-permute-start | bytes 2752520 | tf_op jit(solution)/shard_map/ppermute | solution.py:37
  244.8 19.0 %collective-permute-start.18 = (bf16[2304,256]{1,0:T(8,128)(2,1)}, bf16[2304,256]{1,0:T(8,128)(2,1)}, u32[]{:S(2)}, u32[]{:S(2)}) collective-permute-start(bf16[2304,256]{1,0:T(8,128)(2,1)} %collective-permute-done.17), channel_id=1, source_target_pairs={{0,1},{1,0},{2,3},{3,2},{4,5},{5,4},{6,7},{7,6},{8,9},{9,8},{10,11... | collective-permute-start | bytes 3538952 | tf_op jit(solution)/shard_map/ppermute | solution.py:37
  249.5 3.9 %copy-start.4 = (bf16[576,1024]{1,0:T(8,128)(2,1)}, bf16[576,1024]{1,0:T(8,128)(2,1)S(1)}, u32[]{:S(2)}) copy-start(bf16[576,1024]{1,0:T(8,128)(2,1)S(1)} %multiply_convert_fusion.2) | copy-start | bytes 3538948
  253.4 36.4 %all-to-all-start.2 = ((bf16[8,72,1792]{2,1,0:T(8,128)(2,1)}), bf16[8,72,1792]{2,1,0:T(8,128)(2,1)S(1)}, u32[]{:S(2)}, u32[]{:S(2)}) async-start(bf16[8,72,1792]{2,1,0:T(8,128)(2,1)} %bitcast.57), calls=%async_computation.2 | async-start | bytes 4128768 | tf_op jit(solution)/shard_map/all_to_all | solution.py:31
  289.8 1.3 copy-start.1
  291.1 37.5 %all-to-all-start.1 = ((bf16[8,72,2304]{2,1,0:T(8,128)(2,1)}), bf16[8,72,2304]{2,1,0:T(8,128)(2,1)}, u32[]{:S(2)}, u32[]{:S(2)}) async-start(bf16[8,72,2304]{2,1,0:T(8,128)(2,1)} %bitcast.12), calls=%async_computation.1 | async-start | bytes 5308416 | tf_op jit(solution)/shard_map/all_to_all | solution.py:31
  300.1 7.4 %collective-permute-start.4 = (bf16[48,1792]{1,0:T(8,128)(2,1)}, bf16[48,1792]{1,0:T(8,128)(2,1)S(1)}, u32[]{:S(2)}, u32[]{:S(2)}) collective-permute-start(bf16[48,1792]{1,0:T(8,128)(2,1)} %get-tuple-element.466), channel_id=1, source_target_pairs={{0,112},{16,0},{32,16},{48,32},{64,48},{80,64},{96,80},{112,96},{1... | collective-permute-start | bytes 516104 | tf_op jit(solution)/shard_map/while/body/eval_jaxpr/ppermute | solution.py:41
  301.8 8.2 %collective-permute-start.5 = (bf16[48,1792]{1,0:T(8,128)(2,1)S(1)}, bf16[48,1792]{1,0:T(8,128)(2,1)S(1)}, u32[]{:S(2)}, u32[]{:S(2)}) collective-permute-start(bf16[48,1792]{1,0:T(8,128)(2,1)S(1)} %convert_element_type.294), channel_id=1, source_target_pairs={{0,16},{16,32},{32,48},{48,64},{64,80},{80,96},{96,112},{112,0},{1... | collective-permute-start | bytes 516104 | tf_op jit(solution)/shard_map/while/body/eval_jaxpr/ppermute | solution.py:41
  310.0 6.3 %collective-permute-start.4 = (bf16[48,1792]{1,0:T(8,128)(2,1)}, bf16[48,1792]{1,0:T(8,128)(2,1)S(1)}, u32[]{:S(2)}, u32[]{:S(2)}) collective-permute-start(bf16[48,1792]{1,0:T(8,128)(2,1)} %get-tuple-element.466), channel_id=1, source_target_pairs={{0,112},{16,0},{32,16},{48,32},{64,48},{80,64},{96,80},{112,96},{1... | collective-permute-start | bytes 516104 | tf_op jit(solution)/shard_map/while/body/eval_jaxpr/ppermute | solution.py:41
  311.2 7.3 %collective-permute-start.5 = (bf16[48,1792]{1,0:T(8,128)(2,1)S(1)}, bf16[48,1792]{1,0:T(8,128)(2,1)S(1)}, u32[]{:S(2)}, u32[]{:S(2)}) collective-permute-start(bf16[48,1792]{1,0:T(8,128)(2,1)S(1)} %convert_element_type.294), channel_id=1, source_target_pairs={{0,16},{16,32},{32,48},{48,64},{64,80},{80,96},{96,112},{112,0},{1... | collective-permute-start | bytes 516104 | tf_op jit(solution)/shard_map/while/body/eval_jaxpr/ppermute | solution.py:41
  318.6 5.7 %collective-permute-start.4 = (bf16[48,1792]{1,0:T(8,128)(2,1)}, bf16[48,1792]{1,0:T(8,128)(2,1)S(1)}, u32[]{:S(2)}, u32[]{:S(2)}) collective-permute-start(bf16[48,1792]{1,0:T(8,128)(2,1)} %get-tuple-element.466), channel_id=1, source_target_pairs={{0,112},{16,0},{32,16},{48,32},{64,48},{80,64},{96,80},{112,96},{1... | collective-permute-start | bytes 516104 | tf_op jit(solution)/shard_map/while/body/eval_jaxpr/ppermute | solution.py:41
  319.8 6.7 %collective-permute-start.5 = (bf16[48,1792]{1,0:T(8,128)(2,1)S(1)}, bf16[48,1792]{1,0:T(8,128)(2,1)S(1)}, u32[]{:S(2)}, u32[]{:S(2)}) collective-permute-start(bf16[48,1792]{1,0:T(8,128)(2,1)S(1)} %convert_element_type.294), channel_id=1, source_target_pairs={{0,16},{16,32},{32,48},{48,64},{64,80},{80,96},{96,112},{112,0},{1... | collective-permute-start | bytes 516104 | tf_op jit(solution)/shard_map/while/body/eval_jaxpr/ppermute | solution.py:41
  326.6 34.7 %collective-permute-start.23 = (bf16[48,1792]{1,0:T(8,128)(2,1)}, bf16[48,1792]{1,0:T(8,128)(2,1)}, u32[]{:S(2)}, u32[]{:S(2)}) collective-permute-start(bf16[48,1792]{1,0:T(8,128)(2,1)} %get-tuple-element.313), channel_id=1, source_target_pairs={{0,112},{16,0},{32,16},{48,32},{64,48},{80,64},{96,80},{112,96},{1... | collective-permute-start | bytes 516104 | tf_op jit(solution)/shard_map/ppermute | solution.py:41
  332.0 7.3 %collective-permute-start.2 = (bf16[48,2304]{1,0:T(8,128)(2,1)S(1)}, bf16[48,2304]{1,0:T(8,128)(2,1)S(1)}, u32[]{:S(2)}, u32[]{:S(2)}) collective-permute-start(bf16[48,2304]{1,0:T(8,128)(2,1)S(1)} %get-tuple-element.493), channel_id=1, source_target_pairs={{0,112},{16,0},{32,16},{48,32},{64,48},{80,64},{96,80},{112,96},{1... | collective-permute-start | bytes 663560 | tf_op jit(solution)/shard_map/while/body/eval_jaxpr/ppermute | solution.py:41
  333.8 8.8 %collective-permute-start.3 = (bf16[48,2304]{1,0:T(8,128)(2,1)S(1)}, bf16[48,2304]{1,0:T(8,128)(2,1)S(1)}, u32[]{:S(2)}, u32[]{:S(2)}) collective-permute-start(bf16[48,2304]{1,0:T(8,128)(2,1)S(1)} %convert_element_type.291), channel_id=1, source_target_pairs={{0,16},{16,32},{32,48},{48,64},{64,80},{80,96},{96,112},{112,0},{1... | collective-permute-start | bytes 663560 | tf_op jit(solution)/shard_map/while/body/eval_jaxpr/ppermute | solution.py:41
  342.6 8.0 %collective-permute-start.2 = (bf16[48,2304]{1,0:T(8,128)(2,1)S(1)}, bf16[48,2304]{1,0:T(8,128)(2,1)S(1)}, u32[]{:S(2)}, u32[]{:S(2)}) collective-permute-start(bf16[48,2304]{1,0:T(8,128)(2,1)S(1)} %get-tuple-element.493), channel_id=1, source_target_pairs={{0,112},{16,0},{32,16},{48,32},{64,48},{80,64},{96,80},{112,96},{1... | collective-permute-start | bytes 663560 | tf_op jit(solution)/shard_map/while/body/eval_jaxpr/ppermute | solution.py:41
  342.7 9.3 %collective-permute-start.3 = (bf16[48,2304]{1,0:T(8,128)(2,1)S(1)}, bf16[48,2304]{1,0:T(8,128)(2,1)S(1)}, u32[]{:S(2)}, u32[]{:S(2)}) collective-permute-start(bf16[48,2304]{1,0:T(8,128)(2,1)S(1)} %convert_element_type.291), channel_id=1, source_target_pairs={{0,16},{16,32},{32,48},{48,64},{64,80},{80,96},{96,112},{112,0},{1... | collective-permute-start | bytes 663560 | tf_op jit(solution)/shard_map/while/body/eval_jaxpr/ppermute | solution.py:41
  352.1 7.2 %collective-permute-start.2 = (bf16[48,2304]{1,0:T(8,128)(2,1)S(1)}, bf16[48,2304]{1,0:T(8,128)(2,1)S(1)}, u32[]{:S(2)}, u32[]{:S(2)}) collective-permute-start(bf16[48,2304]{1,0:T(8,128)(2,1)S(1)} %get-tuple-element.493), channel_id=1, source_target_pairs={{0,112},{16,0},{32,16},{48,32},{64,48},{80,64},{96,80},{112,96},{1... | collective-permute-start | bytes 663560 | tf_op jit(solution)/shard_map/while/body/eval_jaxpr/ppermute | solution.py:41
  352.4 8.4 %collective-permute-start.3 = (bf16[48,2304]{1,0:T(8,128)(2,1)S(1)}, bf16[48,2304]{1,0:T(8,128)(2,1)S(1)}, u32[]{:S(2)}, u32[]{:S(2)}) collective-permute-start(bf16[48,2304]{1,0:T(8,128)(2,1)S(1)} %convert_element_type.291), channel_id=1, source_target_pairs={{0,16},{16,32},{32,48},{48,64},{64,80},{80,96},{96,112},{112,0},{1... | collective-permute-start | bytes 663560 | tf_op jit(solution)/shard_map/while/body/eval_jaxpr/ppermute | solution.py:41
  360.9 6.3 %collective-permute-start.19 = (bf16[48,2304]{1,0:T(8,128)(2,1)S(1)}, bf16[48,2304]{1,0:T(8,128)(2,1)S(1)}, u32[]{:S(2)}, u32[]{:S(2)}) collective-permute-start(bf16[48,2304]{1,0:T(8,128)(2,1)S(1)} %get-tuple-element.311), channel_id=1, source_target_pairs={{0,112},{16,0},{32,16},{48,32},{64,48},{80,64},{96,80},{112,96},{1... | collective-permute-start | bytes 663560 | tf_op jit(solution)/shard_map/ppermute | solution.py:41

commit v2 on v1

--- a/solution.py
+++ b/solution.py
@@ -8,9 +8,8 @@
 AXES = ("yl", "z", "x", "yh", "core")
 CAP = 9
 EXTRA = 128
-OUT = (2304, 1792)
-UP = 2048
-LOOPED = (True, True)
+OUT = (1920, 2176)
+HALF = 2048
 
 
 def plane_groups():
@@ -50,26 +49,36 @@
     return parts
 
 
-def summed(blocks, looped):
+def around(own):
+    rows, middle = own.shape[0], NZ // 2
+    whole = jnp.broadcast_to(own[None], (NZ,) + own.shape).reshape(NZ * rows, own.shape[1])
+
+    def turn(hop, state):
+        whole, ahead, behind = state
+        ahead = along_z(ahead, 1)
+        behind = along_z(behind, -1)
+        whole = lax.dynamic_update_slice(whole, behind, (lax.rem(middle + 1 + hop, NZ) * rows, 0))
+        whole = lax.dynamic_update_slice(whole, ahead, ((middle - 1 - hop) * rows, 0))
+        return whole, ahead, behind
+
+    whole = lax.fori_loop(0, middle, turn, (whole, own, own))[0]
+    return with_layout_constraint(whole, Layout(major_to_minor=(0, 1)))
+
+
+def summed(blocks):
     middle = NZ // 2
 
     def turn(hop, state):
         down, up = state
-        down = along_z(down.astype(jnp.bfloat16), -1)
-        up = along_z(up.astype(jnp.bfloat16), 1)
-        down = down.astype(jnp.float32) + blocks[1 + hop].astype(jnp.float32)
-        up = up.astype(jnp.float32) + blocks[NZ - 2 - hop].astype(jnp.float32)
+        down = along_z(down.astype(jnp.bfloat16), -1).astype(jnp.float32)
+        up = along_z(up.astype(jnp.bfloat16), 1).astype(jnp.float32)
+        down = down + blocks[1 + hop].astype(jnp.float32)
+        up = up + jnp.where(hop < middle - 1, blocks[NZ - 1 - hop].astype(jnp.float32), 0.0)
         return down, up
 
-    state = blocks[0].astype(jnp.float32), blocks[NZ - 1].astype(jnp.float32)
-    if looped:
-        state = lax.fori_loop(0, middle - 1, turn, state)
-    else:
-        for hop in range(middle - 1):
-            state = turn(hop, state)
-    down, up = state
-    down = along_z(down.astype(jnp.bfloat16), -1)
-    return (down.astype(jnp.float32) + up).astype(jnp.bfloat16)
+    first = blocks[0].astype(jnp.float32)
+    down, up = lax.fori_loop(0, middle, turn, (first, jnp.zeros_like(first)))
+    return (down + up).astype(jnp.bfloat16)
 
 
 def local(tokens, expert_ids, gate_values, gate_weight, up_weight, down_weight):
@@ -88,27 +97,14 @@
         return jnp.concatenate([own, near, far, hop], axis=1)
 
     gate = pieces(own_gate, 0, width)
-    up0 = pieces(own_up, 0, UP)
-    up1 = pieces(own_up, UP, width - UP)
+    up0 = pieces(own_up, 0, HALF)
+    up1 = pieces(own_up, HALF, width - HALF)
     downs = [pieces(own_down, 0, OUT[0]), pieces(own_down, OUT[0], OUT[1])]
 
     notes = jnp.concatenate([expert_ids.astype(jnp.bfloat16)] + parts_of(gate_values, 2), axis=1)
     notes = jnp.pad(notes, ((0, 0), (0, EXTRA - notes.shape[1])))
-    own = jnp.concatenate([notes, tokens], axis=1)
-    whole = jnp.broadcast_to(own[None], (NZ,) + own.shape).reshape(NZ * rows, own.shape[1])
-
-    def turn(hop, state):
-        whole, ahead, behind = state
-        ahead = along_z(ahead, 1)
-        behind = along_z(behind, -1)
-        whole = lax.dynamic_update_slice(whole, ahead, ((NZ // 2 - 1 - hop) * rows, 0))
-        whole = lax.dynamic_update_slice(whole, behind, ((NZ // 2 + 1 + hop) * rows, 0))
-        return whole, ahead, behind
-
-    whole, ahead, _ = lax.fori_loop(0, NZ // 2 - 1, turn, (whole, own, own))
-    ahead = along_z(ahead, 1)
-    whole = lax.dynamic_update_slice(whole, ahead, (0, 0))
-    whole = with_layout_constraint(whole, Layout(major_to_minor=(0, 1)))
+    whole = around(jnp.concatenate([notes, tokens[:, :HALF]], axis=1))
+    rest = around(tokens[:, HALF:])
 
     count = NZ * rows
     notes = whole[:, : 3 * top].astype(jnp.float32)
@@ -132,18 +128,24 @@
 
     weights = jnp.pad(jnp.concatenate(parts_of(weight, 2), axis=1), ((0, 0), (0, EXTRA - 2 * dests)))
     whole = lax.dynamic_update_slice(whole, weights, (0, 0))
-    packed = lax.dot_general(pack, whole, (((0,), (0,)), ((), ())), preferred_element_type=jnp.float32)
-    packed = packed.astype(jnp.bfloat16).reshape(dests, cap, EXTRA + width)
-    arrived = exchange(packed).reshape(dests * cap, EXTRA + width)
+
+    def sent(block):
+        packed = lax.dot_general(pack, block, (((0,), (0,)), ((), ())), preferred_element_type=jnp.float32)
+        packed = packed.astype(jnp.bfloat16).reshape(dests, cap, block.shape[1])
+        return exchange(packed).reshape(dests * cap, block.shape[1])
+
+    arrived = sent(whole)
+    others = sent(rest)
     mine = lax.axis_index("yl") * NX + lax.axis_index("x")
     weight = arrived[:, : 2 * dests].astype(jnp.float32)
     weight = jnp.where(jnp.arange(2 * dests) % dests == mine, weight, 0.0)
     weight = jnp.sum(weight, axis=1, keepdims=True)
     arrived = arrived[:, EXTRA:]
 
-    gate_part = jnp.dot(arrived, gate, preferred_element_type=jnp.float32)
-    up_part = jnp.dot(arrived[:, :UP], up0, preferred_element_type=jnp.float32)
-    up_part = jnp.dot(arrived[:, UP:], up1, preferred_element_type=jnp.float32) + up_part
+    gate_part = jnp.dot(arrived, gate[:HALF], preferred_element_type=jnp.float32)
+    up_part = jnp.dot(arrived, up0, preferred_element_type=jnp.float32)
+    gate_part = jnp.dot(others, gate[HALF:], preferred_element_type=jnp.float32) + gate_part
+    up_part = jnp.dot(others, up1, preferred_element_type=jnp.float32) + up_part
     hidden = (jax.nn.silu(gate_part) * up_part).astype(jnp.bfloat16)
 
     mixed = []
@@ -153,7 +155,7 @@
         out = exchange(out).reshape(dests * cap, size)
         both = jnp.dot(pack, out, preferred_element_type=jnp.float32)
         both = both.astype(jnp.bfloat16).reshape(NZ, rows, size)
-        mixed.append(summed(both, looped=LOOPED[c]))
+        mixed.append(summed(both))
     return jnp.concatenate(mixed, axis=1)
 
 

time: 369 us -> 328 us (0.89)
  the two profiles are of different devices: /device:TPU:2 before, /device:TPU:14 now
where the time goes in v2:
time: 328 us; the launch traced here: 323 us
  waiting for transfers between devices  154 us (47%)
  starting transfers between devices  93.2 us (28%)
  matrix products  48.1 us (15%)
  local copies, waits for them, and re-layouts  19.1 us (6%)
  other arithmetic  7.88 us (2%)
    ppermute x32, waiting for transfers between devices, along_z(): return lax.ppermute(block, 'z', [(i, (i + step) % NZ) for i in range(NZ)])  71.3 us
    ppermute x15, waiting for transfers between devices, swap(): return lax.ppermute(block, axis, [(0, 1), (1, 0)])  63.8 us
    ppermute x32, starting transfers between devices, along_z(): return lax.ppermute(block, 'z', [(i, (i + step) % NZ) for i in range(NZ)])  56.4 us
    all_to_all x4, starting transfers between devices, exchange(): lax.all_to_all(block, AXES, 0, 0, axis_index_groups=plane_groups(), tiled...  23.9 us
    all_to_all x4, waiting for transfers between devices, exchange(): lax.all_to_all(block, AXES, 0, 0, axis_index_groups=plane_groups(), tiled...  18.8 us
    ppermute x15, starting transfers between devices, swap(): return lax.ppermute(block, axis, [(0, 1), (1, 0)])  13 us
    dot_general x2, matrix products, local(): lax.dot_general(hidden, downs[c], (((1,), (1,)), ((), ())), preferred_ele...  13 us
    dot_general x2, matrix products, sent(): lax.dot_general(pack, block, (((0,), (0,)), ((), ())), preferred_element_...  7.5 us
  transfers between devices with their start and end apart: 51, of which 30 were waited for; matrix products, arithmetic and copies ran while one was open for 19% of the time, Pallas kernels for 0%

profile of v2, /device:TPU:14, one launch (start us, length us, event | category | flops | bytes accessed | tf_op | source)
XLA Modules:
  0.0 323.1 jit_solution(7601857826354675808)
XLA Ops:
  0.0 3.0 slice_bitcast_fusion.2
  3.0 2.3 collective-permute-start.15
  5.7 35.9 %while.70 = (s32[]{:T(128)}, bf16[384,2176]{1,0:T(8,128)(2,1)S(1)}, bf16[48,2176]{1,0:T(8,128)(2,1)S(1)}, bf16[48,2176]{1,0:T(8,128)(2,1)S(1)}, s32[]{:T(128)}, ...) while((s32[]{:T(128)}, bf16[384,2176]{1,0:T(8,128)(2,1)S(1)}, ...), condition=%wide.region_1.2_spmd, body=%wide.region_0.1_spmd.sunk | while | flops 18 | bytes 3342712 | solution.py:64
  5.7 2.0 collective-permute-start.1
  7.7 4.0 %collective-permute-start = (bf16[48,2176]{1,0:T(8,128)(2,1)S(1)}, bf16[48,2176]{1,0:T(8,128)(2,1)S(1)}, u32[]{:S(2)}, u32[]{:S(2)}) collective-permute-start(bf16[48,2176]{1,0:T(8,128)(2,1)S(1)} %get-tuple-element.591), channel_id=1, source_target_pairs={{0,112},{16,0},{32,16},{48,32},{64,48},{80,64},{96,80},{112,96},{1... | collective-permute-start | bytes 626696 | tf_op jit(solution)/shard_map/while/body/eval_jaxpr/ppermute | solution.py:40
  11.7 5.7 %collective-permute-done.1 = bf16[48,2176]{1,0:T(8,128)(2,1)S(1)} collective-permute-done((bf16[48,2176]{1,0:T(8,128)(2,1)S(1)}, bf16[48,2176]{1,0:T(8,128)(2,1)S(1)}, u32[]{:S(2)}, u32[]{:S(2)}) %collective-permute-start.1) | collective-permute-done | bytes 208928 | tf_op jit(solution)/shard_map/while/body/eval_jaxpr/ppermute | solution.py:40
  17.7 3.2 collective-permute-start
  20.9 5.0 %collective-permute-done.1 = bf16[48,2176]{1,0:T(8,128)(2,1)S(1)} collective-permute-done((bf16[48,2176]{1,0:T(8,128)(2,1)S(1)}, bf16[48,2176]{1,0:T(8,128)(2,1)S(1)}, u32[]{:S(2)}, u32[]{:S(2)}) %collective-permute-start.1) | collective-permute-done | bytes 208928 | tf_op jit(solution)/shard_map/while/body/eval_jaxpr/ppermute | solution.py:40
  26.0 1.9 collective-permute-start.1
  29.3 4.1 %collective-permute-done.1 = bf16[48,2176]{1,0:T(8,128)(2,1)S(1)} collective-permute-done((bf16[48,2176]{1,0:T(8,128)(2,1)S(1)}, bf16[48,2176]{1,0:T(8,128)(2,1)S(1)}, u32[]{:S(2)}, u32[]{:S(2)}) %collective-permute-start.1) | collective-permute-done | bytes 208928 | tf_op jit(solution)/shard_map/while/body/eval_jaxpr/ppermute | solution.py:40
  33.8 1.8 collective-permute-start.1
  37.2 3.8 %collective-permute-done.1 = bf16[48,2176]{1,0:T(8,128)(2,1)S(1)} collective-permute-done((bf16[48,2176]{1,0:T(8,128)(2,1)S(1)}, bf16[48,2176]{1,0:T(8,128)(2,1)S(1)}, u32[]{:S(2)}, u32[]{:S(2)}) %collective-permute-start.1) | collective-permute-done | bytes 208928 | tf_op jit(solution)/shard_map/while/body/eval_jaxpr/ppermute | solution.py:40
  42.7 2.9 convolution_convert_fusion
  45.6 5.7 %all-to-all-start.1 = ((bf16[8,72,2176]{2,1,0:T(8,128)(2,1)}), bf16[8,72,2176]{2,1,0:T(8,128)(2,1)S(1)}, u32[]{:S(2)}, u32[]{:S(2)}) async-start(bf16[8,72,2176]{2,1,0:T(8,128)(2,1)} %bitcast.59), calls=%async_computation.1 | async-start | bytes 5013504 | tf_op jit(solution)/shard_map/all_to_all | solution.py:30
  54.1 35.1 %while.71 = (s32[]{:T(128)}, bf16[384,2048]{1,0:T(8,128)(2,1)}, bf16[48,2048]{1,0:T(8,128)(2,1)S(1)}, bf16[48,2048]{1,0:T(8,128)(2,1)S(1)}, s32[]{:T(128)}, /*in...) while((s32[]{:T(128)}, bf16[384,2048]{1,0:T(8,128)(2,1)}, ...), condition=%wide.region_4.5_spmd, body=%wide.region_3.4_spmd.sunk | while | flops 18 | bytes 3146104 | solution.py:64
  54.1 1.8 collective-permute-start.3
  57.3 3.6 %collective-permute-done.3 = bf16[48,2048]{1,0:T(8,128)(2,1)S(1)} collective-permute-done((bf16[48,2048]{1,0:T(8,128)(2,1)S(1)}, bf16[48,2048]{1,0:T(8,128)(2,1)S(1)}, u32[]{:S(2)}, u32[]{:S(2)}) %collective-permute-start.3) | collective-permute-done | bytes 196640 | tf_op jit(solution)/shard_map/while/body/eval_jaxpr/ppermute | solution.py:40
  64.5 1.7 collective-permute-start.2
  66.2 3.6 %collective-permute-done.3 = bf16[48,2048]{1,0:T(8,128)(2,1)S(1)} collective-permute-done((bf16[48,2048]{1,0:T(8,128)(2,1)S(1)}, bf16[48,2048]{1,0:T(8,128)(2,1)S(1)}, u32[]{:S(2)}, u32[]{:S(2)}) %collective-permute-start.3) | collective-permute-done | bytes 196640 | tf_op jit(solution)/shard_map/while/body/eval_jaxpr/ppermute | solution.py:40
  73.1 1.7 collective-permute-start.2
  74.8 4.1 %collective-permute-done.3 = bf16[48,2048]{1,0:T(8,128)(2,1)S(1)} collective-permute-done((bf16[48,2048]{1,0:T(8,128)(2,1)S(1)}, bf16[48,2048]{1,0:T(8,128)(2,1)S(1)}, u32[]{:S(2)}, u32[]{:S(2)}) %collective-permute-start.3) | collective-permute-done | bytes 196640 | tf_op jit(solution)/shard_map/while/body/eval_jaxpr/ppermute | solution.py:40
  82.0 2.1 collective-permute-start.2
  84.2 3.6 %collective-permute-done.3 = bf16[48,2048]{1,0:T(8,128)(2,1)S(1)} collective-permute-done((bf16[48,2048]{1,0:T(8,128)(2,1)S(1)}, bf16[48,2048]{1,0:T(8,128)(2,1)S(1)}, u32[]{:S(2)}, u32[]{:S(2)}) %collective-permute-start.3) | collective-permute-done | bytes 196640 | tf_op jit(solution)/shard_map/while/body/eval_jaxpr/ppermute | solution.py:40
  89.2 2.2 slice_bitcast_fusion.3
  91.9 4.6 %convolution_convert_fusion.1 = bf16[576,2048]{1,0:T(8,128)(2,1)} fusion(pred[384,576]{0,1:T(32,128)(4,1)} %copy-done.6, bf16[384,2048]{1,0:T(8,128)(2,1)} %get-tuple-element.388), kind=kOutput, calls=%fused_computation.52 | convolution fusion | flops 907149312 | bytes 4153344 | tf_op jit(solution)/shard_map/dot_general | solution.py:133
  96.5 16.7 %collective-permute-done.9 = bf16[4096,256]{1,0:T(8,128)(2,1)} collective-permute-done((bf16[4096,256]{1,0:T(8,128)(2,1)}, bf16[4096,256]{1,0:T(8,128)(2,1)}, u32[]{:S(2)}, u32[]{:S(2)}) %collective-permute-start.9) | collective-permute-done | bytes 2097184 | tf_op jit(solution)/shard_map/ppermute | solution.py:36
  114.8 2.8 collective-permute-start.12
  117.8 5.4 %all-to-all-start = ((bf16[8,72,2048]{2,1,0:T(8,128)(2,1)}), bf16[8,72,2048]{2,1,0:T(8,128)(2,1)}, u32[]{:S(2)}, u32[]{:S(2)}) async-start(bf16[8,72,2048]{2,1,0:T(8,128)(2,1)} %bitcast.60), calls=%async_computation | async-start | bytes 4718592 | tf_op jit(solution)/shard_map/all_to_all | solution.py:30
  123.2 6.3 %fusion.21 = f32[576,1024]{1,0:T(8,128)} fusion(bf16[2048,256]{1,0:T(8,128)(2,1)} %collective-permute-done.16, bf16[2048,256]{1,0:T(8,128)(2,1)} %collective-permute-done.15, bf16[2048,256]{1,0:T(8,128)(2,1)} %collective-permute-done.14, bf16[2048,256]{1,0:T(8,128)(2,1)} %get-tuple-element.464, bf16[576,2176]{1,0:T(8,128)(2,1)S(1)} %bitcast.55), kind=kOutput, calls=%fused_computation.36 | convolution fusion | flops 2432696320 | bytes 8912896 | tf_op jit(solution)/shard_map/dot_general | solution.py:146
  131.1 21.1 %collective-permute-done.12 = bf16[2048,256]{1,0:T(8,128)(2,1)} collective-permute-done((bf16[2048,256]{1,0:T(8,128)(2,1)S(1)}, bf16[2048,256]{1,0:T(8,128)(2,1)}, u32[]{:S(2)}, u32[]{:S(2)}) %collective-permute-start.12) | collective-permute-done | bytes 1048608 | tf_op jit(solution)/shard_map/ppermute | solution.py:36
  152.1 4.0 %collective-permute-start.21 = (bf16[2176,256]{1,0:T(8,128)(2,1)}, bf16[2176,256]{1,0:T(8,128)(2,1)}, u32[]{:S(2)}, u32[]{:S(2)}) collective-permute-start(bf16[2176,256]{1,0:T(8,128)(2,1)} %slice_bitcast_fusion), channel_id=1, source_target_pairs={{0,2},{2,0},{1,3},{3,1},{4,6},{6,4},{5,7},{7,5},{8,10},{10,8},{9,1... | collective-permute-start | bytes 3342344 | tf_op jit(solution)/shard_map/ppermute | solution.py:36
  156.1 3.9 %pad_maximum_fusion = bf16[4096,1024]{1,0:T(8,128)(2,1)S(1)} fusion(bf16[4096,256]{1,0:T(8,128)(2,1)} %collective-permute-done.10, bf16[4096,256]{1,0:T(8,128)(2,1)} %collective-permute-done.9, bf16[4096,256]{1,0:T(8,128)(2,1)} %collective-permute-done.8, bf16[4096,256]{1,0:T(8,128)(2,1)S(1)} %bitcast.64), kind=kLoop, calls=%fused_computation.10 | loop fusion | flops 33554432 | bytes 16777216 | tf_op jit(solution)/shard_map/concatenate | solution.py:97
  160.0 3.3 %copy-done = bf16[4096,1024]{1,0:T(8,128)(2,1)} copy-done((bf16[4096,1024]{1,0:T(8,128)(2,1)}, bf16[4096,1024]{1,0:T(8,128)(2,1)S(1)}, u32[]{:S(2)}) %copy-start) | copy-done | bytes 8388632
  163.3 4.0 %fusion.9 = f32[576,1024]{1,0:T(8,128)} fusion(bf16[4096,1024]{1,0:T(8,128)(2,1)S(1)} %pad_maximum_fusion, bf16[576,2176]{1,0:T(8,128)(2,1)S(1)} %bitcast.57), kind=kOutput, calls=%fused_computation.24 | convolution fusion | flops 2415919104 | bytes 8912896 | tf_op jit(solution)/shard_map/dot_general | solution.py:145
  167.4 5.2 %fusion.11 = f32[576,1024]{1,0:T(8,128)S(1)} fusion(bf16[576,2048]{1,0:T(8,128)(2,1)} %bitcast.4, bf16[4096,1024]{1,0:T(8,128)(2,1)} %copy-done), kind=kOutput, calls=%fused_computation.26 | convolution fusion | flops 2415919104 | bytes 8912896 | tf_op jit(solution)/shard_map/dot_general | solution.py:147
  173.2 6.3 %collective-permute-done.18 = bf16[1920,256]{1,0:T(8,128)(2,1)} collective-permute-done((bf16[1920,256]{1,0:T(8,128)(2,1)}, bf16[1920,256]{1,0:T(8,128)(2,1)}, u32[]{:S(2)}, u32[]{:S(2)}) %collective-permute-start.18) | collective-permute-done | bytes 983072 | tf_op jit(solution)/shard_map/ppermute | solution.py:36
  180.0 19.7 %collective-permute-done.21 = bf16[2176,256]{1,0:T(8,128)(2,1)} collective-permute-done((bf16[2176,256]{1,0:T(8,128)(2,1)}, bf16[2176,256]{1,0:T(8,128)(2,1)}, u32[]{:S(2)}, u32[]{:S(2)}) %collective-permute-start.21) | collective-permute-done | bytes 1114144 | tf_op jit(solution)/shard_map/ppermute | solution.py:36
  199.8 5.5 %multiply_convert_fusion.1 = bf16[576,1024]{1,0:T(8,128)(2,1)S(1)} fusion(f32[576,1024]{1,0:T(8,128)S(1)} %copy-done.15, f32[576,1024]{1,0:T(8,128)S(1)} %fusion.11, f32[576,1024]{1,0:T(8,128)S(1)} %copy-done.14, bf16[576,2048]{1,0:T(8,128)(2,1)} %bitcast.4, bf16[2048,256]{1,0:T(8,128)(2,1)} %collective-permute-done.13, ...), kind=kOutput, calls=%fused_computation.55 | convolution fusion | flops 2437414912 | bytes 14811136 | tf_op jit(solution)/shard_map/dot_general | solution.py:148
  205.3 6.0 %multiply_convert_fusion = bf16[576,1920]{1,0:T(8,128)(2,1)} fusion(bf16[576,1024]{1,0:T(8,128)(2,1)S(1)} %multiply_convert_fusion.1, bf16[1920,256]{1,0:T(8,128)(2,1)S(1)} %collective-permute-done.19, bf16[1920,256]{1,0:T(8,128)(2,1)} %collective-permute-done.18, bf16[1920,256]{1,0:T(8,128)(2,1)S(1)} %collective-permute-done.17, ...), kind=kOutput, calls=%fused_computation.22 | convolution fusion | flops 2282864640 | bytes 7325952 | tf_op jit(solution)/shard_map/dot_general | solution.py:153
  211.3 5.8 %all-to-all-start.2 = ((bf16[8,72,1920]{2,1,0:T(8,128)(2,1)}), bf16[8,72,1920]{2,1,0:T(8,128)(2,1)S(1)}, u32[]{:S(2)}, u32[]{:S(2)}) async-start(bf16[8,72,1920]{2,1,0:T(8,128)(2,1)} %bitcast.61), calls=%async_computation.2 | async-start | bytes 4423680 | tf_op jit(solution)/shard_map/all_to_all | solution.py:30
  217.2 7.0 %fusion = bf16[576,2176]{1,0:T(8,128)(2,1)} fusion(bf16[576,1024]{1,0:T(8,128)(2,1)} %copy-done.16, bf16[2176,256]{1,0:T(8,128)(2,1)} %collective-permute-done.22, bf16[2176,256]{1,0:T(8,128)(2,1)} %collective-permute-done.21, bf16[2176,256]{1,0:T(8,128)(2,1)} %collective-permute-done.20, bf16[2176,256]{1,0:T(8,128)(2,1)} %slice_bitcast_fusion, ...), kind=kOutput, calls=%fused_computation.12 | convolution fusion | flops 2587246592 | bytes 8145152 | tf_op jit(solution)/shard_map/dot_general | solution.py:153
  224.2 18.8 %all-to-all-done.2 = bf16[8,72,1920]{2,1,0:T(8,128)(2,1)S(1)} async-done(((bf16[8,72,1920]{2,1,0:T(8,128)(2,1)}), bf16[8,72,1920]{2,1,0:T(8,128)(2,1)S(1)}, u32[]{:S(2)}, u32[]{:S(2)}) %all-to-all-start.2) | async-done | bytes 2211872 | tf_op jit(solution)/shard_map/all_to_all | solution.py:30
  244.4 7.0 %all-to-all-start.3 = ((bf16[8,72,2176]{2,1,0:T(8,128)(2,1)}), bf16[8,72,2176]{2,1,0:T(8,128)(2,1)}, u32[]{:S(2)}, u32[]{:S(2)}) async-start(bf16[8,72,2176]{2,1,0:T(8,128)(2,1)} %bitcast.15), calls=%async_computation.3 | async-start | bytes 5013504 | tf_op jit(solution)/shard_map/all_to_all | solution.py:30
  251.3 3.1 fusion.39
  254.5 30.8 %while.72 = (s32[]{:T(128)}, f32[48,1920]{1,0:T(8,128)S(1)}, f32[48,1920]{1,0:T(8,128)S(1)}, bf16[8,48,1920]{2,1,0:T(8,128)(2,1)S(1)}, s32[]{:T(128)}, /*index=5...) while((s32[]{:T(128)}, f32[48,1920]{1,0:T(8,128)S(1)}, f32[48,1920]{1,0:T(8,128)S(1)}, ...), condition=%wide.region_8.9_spmd.clone, body=%wide.region_7.8_spmd.clone.sunk | while | flops 829451 | bytes 4055337 | solution.py:80
  254.5 2.0 collective-permute-start.4
  258.2 4.1 %collective-permute-done.4 = bf16[48,1920]{1,0:T(8,128)(2,1)S(1)} collective-permute-done((bf16[48,1920]{1,0:T(8,128)(2,1)S(1)}, bf16[48,1920]{1,0:T(8,128)(2,1)S(1)}, u32[]{:S(2)}, u32[]{:S(2)}) %collective-permute-start.4) | collective-permute-done | bytes 184352 | tf_op jit(solution)/shard_map/while/body/eval_jaxpr/ppermute | solution.py:40
  263.2 1.8 collective-permute-start.4
  266.7 3.4 %collective-permute-done.4 = bf16[48,1920]{1,0:T(8,128)(2,1)S(1)} collective-permute-done((bf16[48,1920]{1,0:T(8,128)(2,1)S(1)}, bf16[48,1920]{1,0:T(8,128)(2,1)S(1)}, u32[]{:S(2)}, u32[]{:S(2)}) %collective-permute-start.4) | collective-permute-done | bytes 184352 | tf_op jit(solution)/shard_map/while/body/eval_jaxpr/ppermute | solution.py:40
  271.7 2.5 collective-permute-start.5
  274.3 3.4 %collective-permute-done.4 = bf16[48,1920]{1,0:T(8,128)(2,1)S(1)} collective-permute-done((bf16[48,1920]{1,0:T(8,128)(2,1)S(1)}, bf16[48,1920]{1,0:T(8,128)(2,1)S(1)}, u32[]{:S(2)}, u32[]{:S(2)}) %collective-permute-start.4) | collective-permute-done | bytes 184352 | tf_op jit(solution)/shard_map/while/body/eval_jaxpr/ppermute | solution.py:40
  277.8 1.7 collective-permute-start.4
  279.6 1.8 collective-permute-start.5
  281.4 3.4 %collective-permute-done.4 = bf16[48,1920]{1,0:T(8,128)(2,1)S(1)} collective-permute-done((bf16[48,1920]{1,0:T(8,128)(2,1)S(1)}, bf16[48,1920]{1,0:T(8,128)(2,1)S(1)}, u32[]{:S(2)}, u32[]{:S(2)}) %collective-permute-start.4) | collective-permute-done | bytes 184352 | tf_op jit(solution)/shard_map/while/body/eval_jaxpr/ppermute | solution.py:40
  285.4 3.3 %fusion.8 = bf16[384,2176]{1,0:T(8,128)(2,1)S(1)} fusion(bf16[8,72,2176]{2,1,0:T(8,128)(2,1)} %all-to-all-done.3, s32[8,72]{1,0:T(8,128)S(1)} %multiply_add_fusion, s32[384,8]{0,1:T(8,128)S(1)} %copy-done.8), kind=kOutput, calls=%fused_computation.23 | convolution fusion | flops 963649536 | bytes 4192512 | tf_op jit(solution)/shard_map/dot_general | solution.py:156
  288.8 33.5 %while.73 = (s32[]{:T(128)}, f32[48,2176]{1,0:T(8,128)S(1)}, f32[48,2176]{1,0:T(8,128)S(1)}, bf16[8,48,2176]{2,1,0:T(8,128)(2,1)S(1)}, s32[]{:T(128)}, /*index=5...) while((s32[]{:T(128)}, f32[48,2176]{1,0:T(8,128)S(1)}, f32[48,2176]{1,0:T(8,128)S(1)}, ...), condition=%wide.region_10.11_spmd.clone, body=%wide.region_9.10_spmd.clone.sunk | while | flops 940043 | bytes 4596009 | solution.py:80
  290.3 1.9 collective-permute-start.7
  292.2 5.5 %collective-permute-done.6 = bf16[48,2176]{1,0:T(8,128)(2,1)S(1)} collective-permute-done((bf16[48,2176]{1,0:T(8,128)(2,1)S(1)}, bf16[48,2176]{1,0:T(8,128)(2,1)S(1)}, u32[]{:S(2)}, u32[]{:S(2)}) %collective-permute-start.6) | collective-permute-done | bytes 208928 | tf_op jit(solution)/shard_map/while/body/eval_jaxpr/ppermute | solution.py:40
  299.6 2.2 collective-permute-start.7
  301.8 5.2 %collective-permute-done.6 = bf16[48,2176]{1,0:T(8,128)(2,1)S(1)} collective-permute-done((bf16[48,2176]{1,0:T(8,128)(2,1)S(1)}, bf16[48,2176]{1,0:T(8,128)(2,1)S(1)}, u32[]{:S(2)}, u32[]{:S(2)}) %collective-permute-start.6) | collective-permute-done | bytes 208928 | tf_op jit(solution)/shard_map/while/body/eval_jaxpr/ppermute | solution.py:40
  308.1 2.5 collective-permute-start.7
  310.6 4.4 %collective-permute-done.6 = bf16[48,2176]{1,0:T(8,128)(2,1)S(1)} collective-permute-done((bf16[48,2176]{1,0:T(8,128)(2,1)S(1)}, bf16[48,2176]{1,0:T(8,128)(2,1)S(1)}, u32[]{:S(2)}, u32[]{:S(2)}) %collective-permute-start.6) | collective-permute-done | bytes 208928 | tf_op jit(solution)/shard_map/while/body/eval_jaxpr/ppermute | solution.py:40
  316.3 2.3 collective-permute-start.7
  318.5 3.7 %collective-permute-done.6 = bf16[48,2176]{1,0:T(8,128)(2,1)S(1)} collective-permute-done((bf16[48,2176]{1,0:T(8,128)(2,1)S(1)}, bf16[48,2176]{1,0:T(8,128)(2,1)S(1)}, u32[]{:S(2)}, u32[]{:S(2)}) %collective-permute-start.6) | collective-permute-done | bytes 208928 | tf_op jit(solution)/shard_map/while/body/eval_jaxpr/ppermute | solution.py:40
  (180 shorter events, 40.7 us)
Async XLA Ops:
  0.0 5.3 %copy-start.12 = (f32[48,8]{0,1:T(8,128)S(1)}, f32[48,8]{0,1:T(8,128)}, u32[]{:S(2)}) copy-start(f32[48,8]{0,1:T(8,128)} %param.16) | copy-start | bytes 4612
  0.0 5.4 %copy-start.11 = (s32[48,8]{0,1:T(8,128)S(1)}, s32[48,8]{0,1:T(8,128)}, u32[]{:S(2)}) copy-start(s32[48,8]{0,1:T(8,128)} %param.15) | copy-start | bytes 4612
  0.0 5.5 %copy-start.5 = (bf16[48,4096]{1,0:T(8,128)(2,1)S(1)}, bf16[48,4096]{1,0:T(8,128)(2,1)}, u32[]{:S(2)}) copy-start(bf16[48,4096]{1,0:T(8,128)(2,1)} %param.14) | copy-start | bytes 1179652
  3.0 88.4 %collective-permute-start.15 = (bf16[2048,256]{1,0:T(8,128)(2,1)}, bf16[2048,256]{1,0:T(8,128)(2,1)}, u32[]{:S(2)}, u32[]{:S(2)}) collective-permute-start(bf16[2048,256]{1,0:T(8,128)(2,1)} %get-tuple-element.464), channel_id=1, source_target_pairs={{0,2},{2,0},{1,3},{3,1},{4,6},{6,4},{5,7},{7,5},{8,10},{10,8},{9,1... | collective-permute-start | bytes 3145736 | tf_op jit(solution)/shard_map/ppermute | solution.py:36
  5.3 112.2 %collective-permute-start.14 = (bf16[2048,256]{1,0:T(8,128)(2,1)}, bf16[2048,256]{1,0:T(8,128)(2,1)}, u32[]{:S(2)}, u32[]{:S(2)}) collective-permute-start(bf16[2048,256]{1,0:T(8,128)(2,1)} %get-tuple-element.464), channel_id=1, source_target_pairs={{0,1},{1,0},{2,3},{3,2},{4,5},{5,4},{6,7},{7,6},{8,9},{9,8},{10,11... | collective-permute-start | bytes 3145736 | tf_op jit(solution)/shard_map/ppermute | solution.py:36
  5.7 11.8 %collective-permute-start.1 = (bf16[48,2176]{1,0:T(8,128)(2,1)S(1)}, bf16[48,2176]{1,0:T(8,128)(2,1)S(1)}, u32[]{:S(2)}, u32[]{:S(2)}) collective-permute-start(bf16[48,2176]{1,0:T(8,128)(2,1)S(1)} %get-tuple-element.590), channel_id=1, source_target_pairs={{0,16},{16,32},{32,48},{48,64},{64,80},{80,96},{96,112},{112,0},{1... | collective-permute-start | bytes 626696 | tf_op jit(solution)/shard_map/while/body/eval_jaxpr/ppermute | solution.py:40
  7.7 9.8 %collective-permute-start = (bf16[48,2176]{1,0:T(8,128)(2,1)S(1)}, bf16[48,2176]{1,0:T(8,128)(2,1)S(1)}, u32[]{:S(2)}, u32[]{:S(2)}) collective-permute-start(bf16[48,2176]{1,0:T(8,128)(2,1)S(1)} %get-tuple-element.591), channel_id=1, source_target_pairs={{0,112},{16,0},{32,16},{48,32},{64,48},{80,64},{96,80},{112,96},{1... | collective-permute-start | bytes 626696 | tf_op jit(solution)/shard_map/while/body/eval_jaxpr/ppermute | solution.py:40
  17.6 8.3 %collective-permute-start.1 = (bf16[48,2176]{1,0:T(8,128)(2,1)S(1)}, bf16[48,2176]{1,0:T(8,128)(2,1)S(1)}, u32[]{:S(2)}, u32[]{:S(2)}) collective-permute-start(bf16[48,2176]{1,0:T(8,128)(2,1)S(1)} %get-tuple-element.590), channel_id=1, source_target_pairs={{0,16},{16,32},{32,48},{48,64},{64,80},{80,96},{96,112},{112,0},{1... | collective-permute-start | bytes 626696 | tf_op jit(solution)/shard_map/while/body/eval_jaxpr/ppermute | solution.py:40
  17.7 8.2 %collective-permute-start = (bf16[48,2176]{1,0:T(8,128)(2,1)S(1)}, bf16[48,2176]{1,0:T(8,128)(2,1)S(1)}, u32[]{:S(2)}, u32[]{:S(2)}) collective-permute-start(bf16[48,2176]{1,0:T(8,128)(2,1)S(1)} %get-tuple-element.591), channel_id=1, source_target_pairs={{0,112},{16,0},{32,16},{48,32},{64,48},{80,64},{96,80},{112,96},{1... | collective-permute-start | bytes 626696 | tf_op jit(solution)/shard_map/while/body/eval_jaxpr/ppermute | solution.py:40
  26.0 7.4 %collective-permute-start.1 = (bf16[48,2176]{1,0:T(8,128)(2,1)S(1)}, bf16[48,2176]{1,0:T(8,128)(2,1)S(1)}, u32[]{:S(2)}, u32[]{:S(2)}) collective-permute-start(bf16[48,2176]{1,0:T(8,128)(2,1)S(1)} %get-tuple-element.590), channel_id=1, source_target_pairs={{0,16},{16,32},{32,48},{48,64},{64,80},{80,96},{96,112},{112,0},{1... | collective-permute-start | bytes 626696 | tf_op jit(solution)/shard_map/while/body/eval_jaxpr/ppermute | solution.py:40
  27.9 5.8 %collective-permute-start = (bf16[48,2176]{1,0:T(8,128)(2,1)S(1)}, bf16[48,2176]{1,0:T(8,128)(2,1)S(1)}, u32[]{:S(2)}, u32[]{:S(2)}) collective-permute-start(bf16[48,2176]{1,0:T(8,128)(2,1)S(1)} %get-tuple-element.591), channel_id=1, source_target_pairs={{0,112},{16,0},{32,16},{48,32},{64,48},{80,64},{96,80},{112,96},{1... | collective-permute-start | bytes 626696 | tf_op jit(solution)/shard_map/while/body/eval_jaxpr/ppermute | solution.py:40
  33.8 7.1 %collective-permute-start.1 = (bf16[48,2176]{1,0:T(8,128)(2,1)S(1)}, bf16[48,2176]{1,0:T(8,128)(2,1)S(1)}, u32[]{:S(2)}, u32[]{:S(2)}) collective-permute-start(bf16[48,2176]{1,0:T(8,128)(2,1)S(1)} %get-tuple-element.590), channel_id=1, source_target_pairs={{0,16},{16,32},{32,48},{48,64},{64,80},{80,96},{96,112},{112,0},{1... | collective-permute-start | bytes 626696 | tf_op jit(solution)/shard_map/while/body/eval_jaxpr/ppermute | solution.py:40
  35.7 5.8 %collective-permute-start = (bf16[48,2176]{1,0:T(8,128)(2,1)S(1)}, bf16[48,2176]{1,0:T(8,128)(2,1)S(1)}, u32[]{:S(2)}, u32[]{:S(2)}) collective-permute-start(bf16[48,2176]{1,0:T(8,128)(2,1)S(1)} %get-tuple-element.591), channel_id=1, source_target_pairs={{0,112},{16,0},{32,16},{48,32},{64,48},{80,64},{96,80},{112,96},{1... | collective-permute-start | bytes 626696 | tf_op jit(solution)/shard_map/while/body/eval_jaxpr/ppermute | solution.py:40
  45.6 72.2 %all-to-all-start.1 = ((bf16[8,72,2176]{2,1,0:T(8,128)(2,1)}), bf16[8,72,2176]{2,1,0:T(8,128)(2,1)S(1)}, u32[]{:S(2)}, u32[]{:S(2)}) async-start(bf16[8,72,2176]{2,1,0:T(8,128)(2,1)} %bitcast.59), calls=%async_computation.1 | async-start | bytes 5013504 | tf_op jit(solution)/shard_map/all_to_all | solution.py:30
  51.3 61.9 %collective-permute-start.9 = (bf16[4096,256]{1,0:T(8,128)(2,1)}, bf16[4096,256]{1,0:T(8,128)(2,1)}, u32[]{:S(2)}, u32[]{:S(2)}) collective-permute-start(bf16[4096,256]{1,0:T(8,128)(2,1)} %bitcast.62), channel_id=1, source_target_pairs={{0,2},{2,0},{1,3},{3,1},{4,6},{6,4},{5,7},{7,5},{8,10},{10,8},{9,1... | collective-permute-start | bytes 6291464 | tf_op jit(solution)/shard_map/ppermute | solution.py:36
  54.1 6.9 %collective-permute-start.3 = (bf16[48,2048]{1,0:T(8,128)(2,1)S(1)}, bf16[48,2048]{1,0:T(8,128)(2,1)S(1)}, u32[]{:S(2)}, u32[]{:S(2)}) collective-permute-start(bf16[48,2048]{1,0:T(8,128)(2,1)S(1)} %get-tuple-element.623), channel_id=1, source_target_pairs={{0,16},{16,32},{32,48},{48,64},{64,80},{80,96},{96,112},{112,0},{1... | collective-permute-start | bytes 589832 | tf_op jit(solution)/shard_map/while/body/eval_jaxpr/ppermute | solution.py:40
  55.9 5.7 %collective-permute-start.2 = (bf16[48,2048]{1,0:T(8,128)(2,1)S(1)}, bf16[48,2048]{1,0:T(8,128)(2,1)S(1)}, u32[]{:S(2)}, u32[]{:S(2)}) collective-permute-start(bf16[48,2048]{1,0:T(8,128)(2,1)S(1)} %get-tuple-element.624), channel_id=1, source_target_pairs={{0,112},{16,0},{32,16},{48,32},{64,48},{80,64},{96,80},{112,96},{1... | collective-permute-start | bytes 589832 | tf_op jit(solution)/shard_map/while/body/eval_jaxpr/ppermute | solution.py:40
  63.0 6.9 %collective-permute-start.3 = (bf16[48,2048]{1,0:T(8,128)(2,1)S(1)}, bf16[48,2048]{1,0:T(8,128)(2,1)S(1)}, u32[]{:S(2)}, u32[]{:S(2)}) collective-permute-start(bf16[48,2048]{1,0:T(8,128)(2,1)S(1)} %get-tuple-element.623), channel_id=1, source_target_pairs={{0,16},{16,32},{32,48},{48,64},{64,80},{80,96},{96,112},{112,0},{1... | collective-permute-start | bytes 589832 | tf_op jit(solution)/shard_map/while/body/eval_jaxpr/ppermute | solution.py:40
  64.5 5.7 %collective-permute-start.2 = (bf16[48,2048]{1,0:T(8,128)(2,1)S(1)}, bf16[48,2048]{1,0:T(8,128)(2,1)S(1)}, u32[]{:S(2)}, u32[]{:S(2)}) collective-permute-start(bf16[48,2048]{1,0:T(8,128)(2,1)S(1)} %get-tuple-element.624), channel_id=1, source_target_pairs={{0,112},{16,0},{32,16},{48,32},{64,48},{80,64},{96,80},{112,96},{1... | collective-permute-start | bytes 589832 | tf_op jit(solution)/shard_map/while/body/eval_jaxpr/ppermute | solution.py:40
  71.6 7.4 %collective-permute-start.3 = (bf16[48,2048]{1,0:T(8,128)(2,1)S(1)}, bf16[48,2048]{1,0:T(8,128)(2,1)S(1)}, u32[]{:S(2)}, u32[]{:S(2)}) collective-permute-start(bf16[48,2048]{1,0:T(8,128)(2,1)S(1)} %get-tuple-element.623), channel_id=1, source_target_pairs={{0,16},{16,32},{32,48},{48,64},{64,80},{80,96},{96,112},{112,0},{1... | collective-permute-start | bytes 589832 | tf_op jit(solution)/shard_map/while/body/eval_jaxpr/ppermute | solution.py:40
  73.1 6.4 %collective-permute-start.2 = (bf16[48,2048]{1,0:T(8,128)(2,1)S(1)}, bf16[48,2048]{1,0:T(8,128)(2,1)S(1)}, u32[]{:S(2)}, u32[]{:S(2)}) collective-permute-start(bf16[48,2048]{1,0:T(8,128)(2,1)S(1)} %get-tuple-element.624), channel_id=1, source_target_pairs={{0,112},{16,0},{32,16},{48,32},{64,48},{80,64},{96,80},{112,96},{1... | collective-permute-start | bytes 589832 | tf_op jit(solution)/shard_map/while/body/eval_jaxpr/ppermute | solution.py:40
  80.9 6.9 %collective-permute-start.3 = (bf16[48,2048]{1,0:T(8,128)(2,1)S(1)}, bf16[48,2048]{1,0:T(8,128)(2,1)S(1)}, u32[]{:S(2)}, u32[]{:S(2)}) collective-permute-start(bf16[48,2048]{1,0:T(8,128)(2,1)S(1)} %get-tuple-element.623), channel_id=1, source_target_pairs={{0,16},{16,32},{32,48},{48,64},{64,80},{80,96},{96,112},{112,0},{1... | collective-permute-start | bytes 589832 | tf_op jit(solution)/shard_map/while/body/eval_jaxpr/ppermute | solution.py:40
  82.0 5.8 %collective-permute-start.2 = (bf16[48,2048]{1,0:T(8,128)(2,1)S(1)}, bf16[48,2048]{1,0:T(8,128)(2,1)S(1)}, u32[]{:S(2)}, u32[]{:S(2)}) collective-permute-start(bf16[48,2048]{1,0:T(8,128)(2,1)S(1)} %get-tuple-element.624), channel_id=1, source_target_pairs={{0,112},{16,0},{32,16},{48,32},{64,48},{80,64},{96,80},{112,96},{1... | collective-permute-start | bytes 589832 | tf_op jit(solution)/shard_map/while/body/eval_jaxpr/ppermute | solution.py:40
  89.2 66.9 %collective-permute-start.8 = (bf16[4096,256]{1,0:T(8,128)(2,1)}, bf16[4096,256]{1,0:T(8,128)(2,1)}, u32[]{:S(2)}, u32[]{:S(2)}) collective-permute-start(bf16[4096,256]{1,0:T(8,128)(2,1)} %bitcast.63), channel_id=1, source_target_pairs={{0,1},{1,0},{2,3},{3,2},{4,5},{5,4},{6,7},{7,6},{8,9},{9,8},{10,11... | collective-permute-start | bytes 6291464 | tf_op jit(solution)/shard_map/ppermute | solution.py:36
  91.4 31.8 %collective-permute-start.16 = (bf16[2048,256]{1,0:T(8,128)(2,1)}, bf16[2048,256]{1,0:T(8,128)(2,1)}, u32[]{:S(2)}, u32[]{:S(2)}) collective-permute-start(bf16[2048,256]{1,0:T(8,128)(2,1)} %collective-permute-done.15), channel_id=1, source_target_pairs={{0,1},{1,0},{2,3},{3,2},{4,5},{5,4},{6,7},{7,6},{8,9},{9,8},{10,11... | collective-permute-start | bytes 3145736 | tf_op jit(solution)/shard_map/ppermute | solution.py:36
  91.9 21.8 %copy-start.2 = (bf16[1,4096,256]{2,1,0:T(8,128)(2,1)S(1)}, bf16[1,4096,256]{2,1,0:T(8,128)(2,1)}, u32[]{:S(2)}) copy-start(bf16[1,4096,256]{2,1,0:T(8,128)(2,1)} %param.19) | copy-start | bytes 6291460
  91.9 22.8 %copy-start.4 = (bf16[2048,256]{1,0:T(8,128)(2,1)S(1)}, bf16[2048,256]{1,0:T(8,128)(2,1)}, u32[]{:S(2)}) copy-start(bf16[2048,256]{1,0:T(8,128)(2,1)} %get-tuple-element.463) | copy-start | bytes 3145732
  113.2 42.9 %collective-permute-start.10 = (bf16[4096,256]{1,0:T(8,128)(2,1)}, bf16[4096,256]{1,0:T(8,128)(2,1)}, u32[]{:S(2)}, u32[]{:S(2)}) collective-permute-start(bf16[4096,256]{1,0:T(8,128)(2,1)} %collective-permute-done.9), channel_id=1, source_target_pairs={{0,1},{1,0},{2,3},{3,2},{4,5},{5,4},{6,7},{7,6},{8,9},{9,8},{10,11... | collective-permute-start | bytes 6291464 | tf_op jit(solution)/shard_map/ppermute | solution.py:36
  114.8 37.3 %collective-permute-start.12 = (bf16[2048,256]{1,0:T(8,128)(2,1)S(1)}, bf16[2048,256]{1,0:T(8,128)(2,1)}, u32[]{:S(2)}, u32[]{:S(2)}) collective-permute-start(bf16[2048,256]{1,0:T(8,128)(2,1)S(1)} %copy-done.4), channel_id=1, source_target_pairs={{0,2},{2,0},{1,3},{3,1},{4,6},{6,4},{5,7},{7,5},{8,10},{10,8},{9,1... | collective-permute-start | bytes 3145736 | tf_op jit(solution)/shard_map/ppermute | solution.py:36
  117.6 62.0 %collective-permute-start.11 = (bf16[2048,256]{1,0:T(8,128)(2,1)S(1)}, bf16[2048,256]{1,0:T(8,128)(2,1)}, u32[]{:S(2)}, u32[]{:S(2)}) collective-permute-start(bf16[2048,256]{1,0:T(8,128)(2,1)S(1)} %copy-done.4), channel_id=1, source_target_pairs={{0,1},{1,0},{2,3},{3,2},{4,5},{5,4},{6,7},{7,6},{8,9},{9,8},{10,11... | collective-permute-start | bytes 3145736 | tf_op jit(solution)/shard_map/ppermute | solution.py:36
  117.8 49.6 %all-to-all-start = ((bf16[8,72,2048]{2,1,0:T(8,128)(2,1)}), bf16[8,72,2048]{2,1,0:T(8,128)(2,1)}, u32[]{:S(2)}, u32[]{:S(2)}) async-start(bf16[8,72,2048]{2,1,0:T(8,128)(2,1)} %bitcast.60), calls=%async_computation | async-start | bytes 4718592 | tf_op jit(solution)/shard_map/all_to_all | solution.py:30
  123.2 6.3 %copy-start.13 = (pred[16]{0:T(512)(128)(4,1)S(1)}, pred[16]{0:T(512)(128)(4,1)}, u32[]{:S(2)}) copy-start(pred[16]{0:T(512)(128)(4,1)} %fusion.58) | copy-start | bytes 52
  123.2 32.9 %copy-start.3 = (bf16[1,4096,256]{2,1,0:T(8,128)(2,1)S(1)}, bf16[1,4096,256]{2,1,0:T(8,128)(2,1)}, u32[]{:S(2)}) copy-start(bf16[1,4096,256]{2,1,0:T(8,128)(2,1)} %param.17) | copy-start | bytes 6291460
  130.3 49.2 %collective-permute-start.18 = (bf16[1920,256]{1,0:T(8,128)(2,1)}, bf16[1920,256]{1,0:T(8,128)(2,1)}, u32[]{:S(2)}, u32[]{:S(2)}) collective-permute-start(bf16[1920,256]{1,0:T(8,128)(2,1)} %slice_bitcast_fusion.3), channel_id=1, source_target_pairs={{0,2},{2,0},{1,3},{3,1},{4,6},{6,4},{5,7},{7,5},{8,10},{10,8},{9,1... | collective-permute-start | bytes 2949128 | tf_op jit(solution)/shard_map/ppermute | solution.py:36
  152.1 47.6 %collective-permute-start.21 = (bf16[2176,256]{1,0:T(8,128)(2,1)}, bf16[2176,256]{1,0:T(8,128)(2,1)}, u32[]{:S(2)}, u32[]{:S(2)}) collective-permute-start(bf16[2176,256]{1,0:T(8,128)(2,1)} %slice_bitcast_fusion), channel_id=1, source_target_pairs={{0,2},{2,0},{1,3},{3,1},{4,6},{6,4},{5,7},{7,5},{8,10},{10,8},{9,1... | collective-permute-start | bytes 3342344 | tf_op jit(solution)/shard_map/ppermute | solution.py:36
  156.1 43.7 %collective-permute-start.13 = (bf16[2048,256]{1,0:T(8,128)(2,1)}, bf16[2048,256]{1,0:T(8,128)(2,1)}, u32[]{:S(2)}, u32[]{:S(2)}) collective-permute-start(bf16[2048,256]{1,0:T(8,128)(2,1)} %collective-permute-done.12), channel_id=1, source_target_pairs={{0,1},{1,0},{2,3},{3,2},{4,5},{5,4},{6,7},{7,6},{8,9},{9,8},{10,11... | collective-permute-start | bytes 3145736 | tf_op jit(solution)/shard_map/ppermute | solution.py:36
  167.4 32.4 %copy-start.14 = (f32[576,1024]{1,0:T(8,128)S(1)}, f32[576,1024]{1,0:T(8,128)}, u32[]{:S(2)}) copy-start(f32[576,1024]{1,0:T(8,128)} %fusion.9) | copy-start | bytes 7077892
  167.4 32.4 %copy-start.15 = (f32[576,1024]{1,0:T(8,128)S(1)}, f32[576,1024]{1,0:T(8,128)}, u32[]{:S(2)}) copy-start(f32[576,1024]{1,0:T(8,128)} %fusion.21) | copy-start | bytes 7077892
  172.6 32.7 %copy-start.9 = (f32[576]{0:T(1024)S(1)}, f32[576]{0:T(1024)}, u32[]{:S(2)}) copy-start(f32[576]{0:T(1024)} %select_reduce_fusion) | copy-start | bytes 6916
  172.6 32.7 %collective-permute-start.17 = (bf16[1920,256]{1,0:T(8,128)(2,1)}, bf16[1920,256]{1,0:T(8,128)(2,1)S(1)}, u32[]{:S(2)}, u32[]{:S(2)}) collective-permute-start(bf16[1920,256]{1,0:T(8,128)(2,1)} %slice_bitcast_fusion.3), channel_id=1, source_target_pairs={{0,1},{1,0},{2,3},{3,2},{4,5},{5,4},{6,7},{7,6},{8,9},{9,8},{10,11... | collective-permute-start | bytes 2949128 | tf_op jit(solution)/shard_map/ppermute | solution.py:36
  179.5 37.6 %collective-permute-start.20 = (bf16[2176,256]{1,0:T(8,128)(2,1)}, bf16[2176,256]{1,0:T(8,128)(2,1)}, u32[]{:S(2)}, u32[]{:S(2)}) collective-permute-start(bf16[2176,256]{1,0:T(8,128)(2,1)} %slice_bitcast_fusion), channel_id=1, source_target_pairs={{0,1},{1,0},{2,3},{3,2},{4,5},{5,4},{6,7},{7,6},{8,9},{9,8},{10,11... | collective-permute-start | bytes 3342344 | tf_op jit(solution)/shard_map/ppermute | solution.py:36
  179.5 25.8 %collective-permute-start.19 = (bf16[1920,256]{1,0:T(8,128)(2,1)}, bf16[1920,256]{1,0:T(8,128)(2,1)S(1)}, u32[]{:S(2)}, u32[]{:S(2)}) collective-permute-start(bf16[1920,256]{1,0:T(8,128)(2,1)} %collective-permute-done.18), channel_id=1, source_target_pairs={{0,1},{1,0},{2,3},{3,2},{4,5},{5,4},{6,7},{7,6},{8,9},{9,8},{10,11... | collective-permute-start | bytes 2949128 | tf_op jit(solution)/shard_map/ppermute | solution.py:36
  199.8 17.4 %collective-permute-start.22 = (bf16[2176,256]{1,0:T(8,128)(2,1)}, bf16[2176,256]{1,0:T(8,128)(2,1)}, u32[]{:S(2)}, u32[]{:S(2)}) collective-permute-start(bf16[2176,256]{1,0:T(8,128)(2,1)} %collective-permute-done.21), channel_id=1, source_target_pairs={{0,1},{1,0},{2,3},{3,2},{4,5},{5,4},{6,7},{7,6},{8,9},{9,8},{10,11... | collective-permute-start | bytes 3342344 | tf_op jit(solution)/shard_map/ppermute | solution.py:36
  205.3 6.0 %copy-start.16 = (bf16[576,1024]{1,0:T(8,128)(2,1)}, bf16[576,1024]{1,0:T(8,128)(2,1)S(1)}, u32[]{:S(2)}) copy-start(bf16[576,1024]{1,0:T(8,128)(2,1)S(1)} %multiply_convert_fusion.1) | copy-start | bytes 3538948
  211.3 5.9 %copy-start.10 = (f32[576]{0:T(1024)S(1)}, f32[576]{0:T(1024)}, u32[]{:S(2)}) copy-start(f32[576]{0:T(1024)} %select_reduce_fusion) | copy-start | bytes 6916
  211.3 31.7 %all-to-all-start.2 = ((bf16[8,72,1920]{2,1,0:T(8,128)(2,1)}), bf16[8,72,1920]{2,1,0:T(8,128)(2,1)S(1)}, u32[]{:S(2)}, u32[]{:S(2)}) async-start(bf16[8,72,1920]{2,1,0:T(8,128)(2,1)} %bitcast.61), calls=%async_computation.2 | async-start | bytes 4423680 | tf_op jit(solution)/shard_map/all_to_all | solution.py:30
  243.0 8.3 %copy-start.8 = (s32[384,8]{0,1:T(8,128)S(1)}, s32[384,8]{0,1:T(8,128)}, u32[]{:S(2)}) copy-start(s32[384,8]{0,1:T(8,128)} %copy-done.7) | copy-start | bytes 36868
  244.4 41.0 %all-to-all-start.3 = ((bf16[8,72,2176]{2,1,0:T(8,128)(2,1)}), bf16[8,72,2176]{2,1,0:T(8,128)(2,1)}, u32[]{:S(2)}, u32[]{:S(2)}) async-start(bf16[8,72,2176]{2,1,0:T(8,128)(2,1)} %bitcast.15), calls=%async_computation.3 | async-start | bytes 5013504 | tf_op jit(solution)/shard_map/all_to_all | solution.py:30
  254.5 7.8 %collective-permute-start.4 = (bf16[48,1920]{1,0:T(8,128)(2,1)S(1)}, bf16[48,1920]{1,0:T(8,128)(2,1)S(1)}, u32[]{:S(2)}, u32[]{:S(2)}) collective-permute-start(bf16[48,1920]{1,0:T(8,128)(2,1)S(1)} %select_convert_fusion.4), channel_id=1, source_target_pairs={{0,16},{16,32},{32,48},{48,64},{64,80},{80,96},{96,112},{112,0},{1... | collective-permute-start | bytes 552968 | tf_op jit(solution)/shard_map/while/body/eval_jaxpr/ppermute | solution.py:40
  256.5 6.6 %collective-permute-start.5 = (bf16[48,1920]{1,0:T(8,128)(2,1)S(1)}, bf16[48,1920]{1,0:T(8,128)(2,1)S(1)}, u32[]{:S(2)}, u32[]{:S(2)}) collective-permute-start(bf16[48,1920]{1,0:T(8,128)(2,1)S(1)} %convert_element_type.278), channel_id=1, source_target_pairs={{0,112},{16,0},{32,16},{48,32},{64,48},{80,64},{96,80},{112,96},{1... | collective-permute-start | bytes 552968 | tf_op jit(solution)/shard_map/while/body/eval_jaxpr/ppermute | solution.py:40
  263.2 6.8 %collective-permute-start.4 = (bf16[48,1920]{1,0:T(8,128)(2,1)S(1)}, bf16[48,1920]{1,0:T(8,128)(2,1)S(1)}, u32[]{:S(2)}, u32[]{:S(2)}) collective-permute-start(bf16[48,1920]{1,0:T(8,128)(2,1)S(1)} %select_convert_fusion.4), channel_id=1, source_target_pairs={{0,16},{16,32},{32,48},{48,64},{64,80},{80,96},{96,112},{112,0},{1... | collective-permute-start | bytes 552968 | tf_op jit(solution)/shard_map/while/body/eval_jaxpr/ppermute | solution.py:40
  265.1 5.6 %collective-permute-start.5 = (bf16[48,1920]{1,0:T(8,128)(2,1)S(1)}, bf16[48,1920]{1,0:T(8,128)(2,1)S(1)}, u32[]{:S(2)}, u32[]{:S(2)}) collective-permute-start(bf16[48,1920]{1,0:T(8,128)(2,1)S(1)} %convert_element_type.278), channel_id=1, source_target_pairs={{0,112},{16,0},{32,16},{48,32},{64,48},{80,64},{96,80},{112,96},{1... | collective-permute-start | bytes 552968 | tf_op jit(solution)/shard_map/while/body/eval_jaxpr/ppermute | solution.py:40
  270.9 6.8 %collective-permute-start.4 = (bf16[48,1920]{1,0:T(8,128)(2,1)S(1)}, bf16[48,1920]{1,0:T(8,128)(2,1)S(1)}, u32[]{:S(2)}, u32[]{:S(2)}) collective-permute-start(bf16[48,1920]{1,0:T(8,128)(2,1)S(1)} %select_convert_fusion.4), channel_id=1, source_target_pairs={{0,16},{16,32},{32,48},{48,64},{64,80},{80,96},{96,112},{112,0},{1... | collective-permute-start | bytes 552968 | tf_op jit(solution)/shard_map/while/body/eval_jaxpr/ppermute | solution.py:40
  271.7 5.9 %collective-permute-start.5 = (bf16[48,1920]{1,0:T(8,128)(2,1)S(1)}, bf16[48,1920]{1,0:T(8,128)(2,1)S(1)}, u32[]{:S(2)}, u32[]{:S(2)}) collective-permute-start(bf16[48,1920]{1,0:T(8,128)(2,1)S(1)} %convert_element_type.278), channel_id=1, source_target_pairs={{0,112},{16,0},{32,16},{48,32},{64,48},{80,64},{96,80},{112,96},{1... | collective-permute-start | bytes 552968 | tf_op jit(solution)/shard_map/while/body/eval_jaxpr/ppermute | solution.py:40
  277.8 6.9 %collective-permute-start.4 = (bf16[48,1920]{1,0:T(8,128)(2,1)S(1)}, bf16[48,1920]{1,0:T(8,128)(2,1)S(1)}, u32[]{:S(2)}, u32[]{:S(2)}) collective-permute-start(bf16[48,1920]{1,0:T(8,128)(2,1)S(1)} %select_convert_fusion.4), channel_id=1, source_target_pairs={{0,16},{16,32},{32,48},{48,64},{64,80},{80,96},{96,112},{112,0},{1... | collective-permute-start | bytes 552968 | tf_op jit(solution)/shard_map/while/body/eval_jaxpr/ppermute | solution.py:40
  279.6 5.6 %collective-permute-start.5 = (bf16[48,1920]{1,0:T(8,128)(2,1)S(1)}, bf16[48,1920]{1,0:T(8,128)(2,1)S(1)}, u32[]{:S(2)}, u32[]{:S(2)}) collective-permute-start(bf16[48,1920]{1,0:T(8,128)(2,1)S(1)} %convert_element_type.278), channel_id=1, source_target_pairs={{0,112},{16,0},{32,16},{48,32},{64,48},{80,64},{96,80},{112,96},{1... | collective-permute-start | bytes 552968 | tf_op jit(solution)/shard_map/while/body/eval_jaxpr/ppermute | solution.py:40
  288.8 8.9 %collective-permute-start.6 = (bf16[48,2176]{1,0:T(8,128)(2,1)S(1)}, bf16[48,2176]{1,0:T(8,128)(2,1)S(1)}, u32[]{:S(2)}, u32[]{:S(2)}) collective-permute-start(bf16[48,2176]{1,0:T(8,128)(2,1)S(1)} %select_convert_fusion.5), channel_id=1, source_target_pairs={{0,16},{16,32},{32,48},{48,64},{64,80},{80,96},{96,112},{112,0},{1... | collective-permute-start | bytes 626696 | tf_op jit(solution)/shard_map/while/body/eval_jaxpr/ppermute | solution.py:40
  290.3 7.9 %collective-permute-start.7 = (bf16[48,2176]{1,0:T(8,128)(2,1)S(1)}, bf16[48,2176]{1,0:T(8,128)(2,1)S(1)}, u32[]{:S(2)}, u32[]{:S(2)}) collective-permute-start(bf16[48,2176]{1,0:T(8,128)(2,1)S(1)} %convert_element_type.281), channel_id=1, source_target_pairs={{0,112},{16,0},{32,16},{48,32},{64,48},{80,64},{96,80},{112,96},{1... | collective-permute-start | bytes 626696 | tf_op jit(solution)/shard_map/while/body/eval_jaxpr/ppermute | solution.py:40
  298.3 8.6 %collective-permute-start.6 = (bf16[48,2176]{1,0:T(8,128)(2,1)S(1)}, bf16[48,2176]{1,0:T(8,128)(2,1)S(1)}, u32[]{:S(2)}, u32[]{:S(2)}) collective-permute-start(bf16[48,2176]{1,0:T(8,128)(2,1)S(1)} %select_convert_fusion.5), channel_id=1, source_target_pairs={{0,16},{16,32},{32,48},{48,64},{64,80},{80,96},{96,112},{112,0},{1... | collective-permute-start | bytes 626696 | tf_op jit(solution)/shard_map/while/body/eval_jaxpr/ppermute | solution.py:40
  299.6 7.4 %collective-permute-start.7 = (bf16[48,2176]{1,0:T(8,128)(2,1)S(1)}, bf16[48,2176]{1,0:T(8,128)(2,1)S(1)}, u32[]{:S(2)}, u32[]{:S(2)}) collective-permute-start(bf16[48,2176]{1,0:T(8,128)(2,1)S(1)} %convert_element_type.281), channel_id=1, source_target_pairs={{0,112},{16,0},{32,16},{48,32},{64,48},{80,64},{96,80},{112,96},{1... | collective-permute-start | bytes 626696 | tf_op jit(solution)/shard_map/while/body/eval_jaxpr/ppermute | solution.py:40
  307.1 7.8 %collective-permute-start.6 = (bf16[48,2176]{1,0:T(8,128)(2,1)S(1)}, bf16[48,2176]{1,0:T(8,128)(2,1)S(1)}, u32[]{:S(2)}, u32[]{:S(2)}) collective-permute-start(bf16[48,2176]{1,0:T(8,128)(2,1)S(1)} %select_convert_fusion.5), channel_id=1, source_target_pairs={{0,16},{16,32},{32,48},{48,64},{64,80},{80,96},{96,112},{112,0},{1... | collective-permute-start | bytes 626696 | tf_op jit(solution)/shard_map/while/body/eval_jaxpr/ppermute | solution.py:40
  308.1 6.8 %collective-permute-start.7 = (bf16[48,2176]{1,0:T(8,128)(2,1)S(1)}, bf16[48,2176]{1,0:T(8,128)(2,1)S(1)}, u32[]{:S(2)}, u32[]{:S(2)}) collective-permute-start(bf16[48,2176]{1,0:T(8,128)(2,1)S(1)} %convert_element_type.281), channel_id=1, source_target_pairs={{0,112},{16,0},{32,16},{48,32},{64,48},{80,64},{96,80},{112,96},{1... | collective-permute-start | bytes 626696 | tf_op jit(solution)/shard_map/while/body/eval_jaxpr/ppermute | solution.py:40
  315.1 7.1 %collective-permute-start.6 = (bf16[48,2176]{1,0:T(8,128)(2,1)S(1)}, bf16[48,2176]{1,0:T(8,128)(2,1)S(1)}, u32[]{:S(2)}, u32[]{:S(2)}) collective-permute-start(bf16[48,2176]{1,0:T(8,128)(2,1)S(1)} %select_convert_fusion.5), channel_id=1, source_target_pairs={{0,16},{16,32},{32,48},{48,64},{64,80},{80,96},{96,112},{112,0},{1... | collective-permute-start | bytes 626696 | tf_op jit(solution)/shard_map/while/body/eval_jaxpr/ppermute | solution.py:40
  316.3 5.9 %collective-permute-start.7 = (bf16[48,2176]{1,0:T(8,128)(2,1)S(1)}, bf16[48,2176]{1,0:T(8,128)(2,1)S(1)}, u32[]{:S(2)}, u32[]{:S(2)}) collective-permute-start(bf16[48,2176]{1,0:T(8,128)(2,1)S(1)} %convert_element_type.281), channel_id=1, source_target_pairs={{0,112},{16,0},{32,16},{48,32},{64,48},{80,64},{96,80},{112,96},{1... | collective-permute-start | bytes 626696 | tf_op jit(solution)/shard_map/while/body/eval_jaxpr/ppermute | solution.py:40
  (4 other events, 10.7 us)
